TPU v7x, 512 devices: a whole 4x8x8 slice. The times are simulated.
512 devices in a mesh: seq: 64 (over x, y, core), ch: 8 (over z).
Axes of the slice: x: 4, y: 8, z: 8, core: 2. Of those that a mesh axis runs over, the one named last changes fastest.
Arguments:
- signal: bfloat16 [256, 32768], P('ch', 'seq'), may hold values from -6 to 6
- in_gate: bfloat16 [256, 32768], P('ch', 'seq'), may hold values from -6 to 6
- out_gate: bfloat16 [256, 32768], P('ch', 'seq'), may hold values from -6 to 6
- short_taps: float32 [256, 128], P('ch'), may hold values from -0.5 to 0.5
- skip_gain: float32 [256], P('ch'), may hold values from 0.5 to 1.5
- decay_rate: float32 [256], P('ch'), may hold values from 9.368896e-05 to 0.00046844484
- embed_weight: float32 [33, 64], replicated, may hold values from -1 to 1
- embed_bias: float32 [64], replicated, may hold values from -3.140625 to 3.140625
- sine_freq: float32 [64], replicated, may hold values from 1 to 10
- mid_weight: float32 [64, 64], replicated, may hold values from -0.75 to 0.75
- mid_bias: float32 [64], replicated, may hold values from -3.140625 to 3.140625
- out_weight: float32 [64, 256], P(None, 'ch'), may hold values from -0.75 to 0.75
Outputs:
- mixed: bfloat16 [256, 32768], P('ch', 'seq')
All inputs are finite; a program needn't handle non-finite values.
Results may differ from a plain program's by a relative error of at most 0.001.
Values may be sent and summed in bfloat16 or wider, within the bound.
A program may use at most 64 MiB of HBM per device.

v0:
```python
import math

import jax
import jax.numpy as jnp
from jax import lax
from jax.sharding import PartitionSpec as P

BANDS = 16


def from_behind(shard, axis, by):
    count = lax.axis_size(axis)
    pairs = [(i, i + by) for i in range(count) if 0 <= i + by < count]
    return lax.ppermute(shard, axis, pairs)


def embed_rows(positions, full_len):
    phase = positions % full_len
    columns = [positions.astype(jnp.float32) / full_len]
    for band in range(BANDS):
        angle = phase.astype(jnp.float32) * (2.0 * math.pi / full_len)
        columns.append(jnp.cos(angle))
        columns.append(jnp.sin(angle))
        phase = 2 * phase % full_len
    return jnp.stack(columns, axis=1)


def filter_hidden(positions, full_len, embed_weight, embed_bias, sine_freq, mid_weight, mid_bias):
    embedding = embed_rows(positions, full_len)
    first = jnp.sin(
        sine_freq
        * (
            jnp.dot(
                embedding,
                embed_weight,
                precision=lax.Precision.HIGHEST,
                preferred_element_type=jnp.float32,
            )
            + embed_bias
        )
    )
    return jnp.sin(
        sine_freq
        * (
            jnp.dot(
                first,
                mid_weight,
                precision=lax.Precision.HIGHEST,
                preferred_element_type=jnp.float32,
            )
            + mid_bias
        )
    )


def shape_filter(second, positions, out_weight, decay_rate):
    raw_vals = jnp.einsum("nf,fc->cn", second, out_weight, precision=lax.Precision.HIGHEST)
    return raw_vals * (
        jnp.sqrt(2.0 * decay_rate)[:, None]
        * jnp.exp(-decay_rate[:, None] * positions.astype(jnp.float32)[None, :])
    )


def angle_table(rows, cols, period):
    product = (
        lax.broadcasted_iota(jnp.int32, (rows, cols), 0)
        * lax.broadcasted_iota(jnp.int32, (rows, cols), 1)
        % period
    )
    angle = product.astype(jnp.float32) * (2.0 * math.pi / period)
    return (jnp.cos(angle), jnp.sin(angle))


def rotate(real_part, imag_part, cos_vals, sin_vals):
    return (
        real_part * cos_vals - imag_part * sin_vals,
        imag_part * cos_vals + real_part * sin_vals,
    )


def twiddle_angle(freq_ids, offsets, fft_len):
    return (freq_ids[:, None] * offsets[None, :]).astype(jnp.float32) * (2.0 * math.pi / fft_len)


def across_blocks(columns, block_cos, block_sin, seq_index, slice_len, fft_len):
    real_part = jnp.einsum("ca,kab->kcb", block_cos, columns, precision=lax.Precision.HIGHEST)
    imag_part = -jnp.einsum("ca,kab->kcb", block_sin, columns, precision=lax.Precision.HIGHEST)
    freq_ids = jnp.arange(block_cos.shape[0], dtype=jnp.int32)
    offsets = seq_index * slice_len + jnp.arange(slice_len, dtype=jnp.int32)
    angle = twiddle_angle(freq_ids, offsets, fft_len)
    return rotate(real_part, imag_part, jnp.cos(angle)[None], -jnp.sin(angle)[None])


def transform_rows(real_part, imag_part, offset_cos, offset_sin, sign):
    shape = real_part.shape
    flat_real = real_part.reshape(-1, shape[-1])
    flat_imag = imag_part.reshape(-1, shape[-1])
    cos_real = jnp.dot(
        flat_real, offset_cos, precision=lax.Precision.HIGHEST, preferred_element_type=jnp.float32
    )
    cos_imag = jnp.dot(
        flat_imag, offset_cos, precision=lax.Precision.HIGHEST, preferred_element_type=jnp.float32
    )
    sin_real = jnp.dot(
        flat_real, offset_sin, precision=lax.Precision.HIGHEST, preferred_element_type=jnp.float32
    )
    sin_imag = jnp.dot(
        flat_imag, offset_sin, precision=lax.Precision.HIGHEST, preferred_element_type=jnp.float32
    )
    return (
        (cos_real - sign * sin_imag).reshape(shape),
        (cos_imag + sign * sin_real).reshape(shape),
    )


def causal_matrix(short_taps):
    channels, tap_count = short_taps.shape
    period = 3 * tap_count
    padding = jnp.zeros((channels, 2 * tap_count - 1), jnp.float32)
    pattern = jnp.concatenate(
        [jnp.zeros((channels, 1), jnp.float32), short_taps[:, ::-1], padding], axis=1
    )
    tiled = jnp.tile(pattern, (1, tap_count))[:, : tap_count * (period - 1)]
    return tiled.reshape(channels, tap_count, period - 1)[:, :, : 2 * tap_count]


def on_device(
    signal,
    in_gate,
    out_gate,
    short_taps,
    skip_gain,
    decay_rate,
    embed_weight,
    embed_bias,
    sine_freq,
    mid_weight,
    mid_bias,
    out_weight,
):
    channels, local_len = signal.shape
    tap_count = short_taps.shape[1]
    seq_devs = lax.axis_size("seq")
    seq_index = lax.axis_index("seq")
    full_len = seq_devs * local_len
    fft_len = 2 * full_len
    slice_len = local_len // seq_devs
    prior_rim = from_behind(signal[:, local_len - tap_count :], "seq", 1)
    blocks = local_len // tap_count
    current = signal.reshape(channels, blocks, tap_count)
    earlier = jnp.concatenate([prior_rim[:, None, :], current[:, :-1, :]], axis=1)
    window = jnp.concatenate([earlier, current], axis=2).astype(jnp.float32)
    toeplitz = causal_matrix(short_taps)
    short_out = jnp.einsum(
        "cij,cbj->cbi", toeplitz, window, precision=lax.Precision.HIGHEST
    ).reshape(channels, local_len)
    gated_in = in_gate.astype(jnp.float32) * short_out
    block_cos, block_sin = angle_table(2 * seq_devs, seq_devs, 2 * seq_devs)
    offset_cos, offset_sin = angle_table(local_len, local_len, local_len)
    own_positions = seq_index * local_len + jnp.arange(local_len, dtype=jnp.int32)
    feat_rows = local_len // lax.axis_size("ch")
    start = seq_index * local_len + lax.axis_index("ch") * feat_rows
    part_rows = filter_hidden(
        start + jnp.arange(feat_rows, dtype=jnp.int32),
        full_len,
        embed_weight,
        embed_bias,
        sine_freq,
        mid_weight,
        mid_bias,
    )
    second = lax.all_gather(part_rows, "ch", axis=0, tiled=True)
    filter_vals = shape_filter(second, own_positions, out_weight, decay_rate)
    signal_cols, filter_cols = (
        lax.all_to_all(
            gated_in.reshape(channels, 1, local_len), "seq", split_axis=2, concat_axis=1, tiled=True
        ),
        lax.all_to_all(
            filter_vals.reshape(channels, 1, local_len),
            "seq",
            split_axis=2,
            concat_axis=1,
            tiled=True,
        ),
    )
    signal_real, signal_imag = across_blocks(
        signal_cols, block_cos, block_sin, seq_index, slice_len, fft_len
    )
    filt_real, filt_imag = across_blocks(
        filter_cols, block_cos, block_sin, seq_index, slice_len, fft_len
    )
    signal_real, signal_imag, filt_real, filt_imag = (
        lax.all_to_all(signal_real, "seq", split_axis=1, concat_axis=2, tiled=True),
        lax.all_to_all(signal_imag, "seq", split_axis=1, concat_axis=2, tiled=True),
        lax.all_to_all(filt_real, "seq", split_axis=1, concat_axis=2, tiled=True),
        lax.all_to_all(filt_imag, "seq", split_axis=1, concat_axis=2, tiled=True),
    )
    signal_real, signal_imag = transform_rows(
        signal_real, signal_imag, offset_cos, offset_sin, -1.0
    )
    filt_real, filt_imag = transform_rows(filt_real, filt_imag, offset_cos, offset_sin, -1.0)
    prod_real = signal_real * filt_real - signal_imag * filt_imag
    prod_imag = signal_real * filt_imag + signal_imag * filt_real
    back_real, back_imag = transform_rows(prod_real, prod_imag, offset_cos, offset_sin, 1.0)
    own_freqs = 2 * seq_index + jnp.arange(2, dtype=jnp.int32)
    angle = twiddle_angle(own_freqs, jnp.arange(local_len, dtype=jnp.int32), fft_len)
    back_real, back_imag = rotate(back_real, back_imag, jnp.cos(angle)[None], jnp.sin(angle)[None])
    back_real, back_imag = (
        lax.all_to_all(back_real, "seq", split_axis=2, concat_axis=1, tiled=True),
        lax.all_to_all(back_imag, "seq", split_axis=2, concat_axis=1, tiled=True),
    )
    result = (
        jnp.einsum("ca,kcb->kab", block_cos, back_real, precision=lax.Precision.HIGHEST)
        - jnp.einsum("ca,kcb->kab", block_sin, back_imag, precision=lax.Precision.HIGHEST)
    ) * (1.0 / fft_len)
    conv = lax.all_to_all(result, "seq", split_axis=1, concat_axis=2, tiled=True).reshape(
        channels, local_len
    )
    return (out_gate.astype(jnp.float32) * (conv + skip_gain[:, None] * gated_in)).astype(
        jnp.bfloat16
    )


def solution(mesh):
    in_specs = (
        P("ch", "seq"),
        P("ch", "seq"),
        P("ch", "seq"),
        P("ch", None),
        P("ch"),
        P("ch"),
        P(),
        P(),
        P(),
        P(),
        P(),
        P(None, "ch"),
    )
    out_specs = P("ch", "seq")
    return jax.shard_map(
        on_device, mesh=mesh, in_specs=in_specs, out_specs=out_specs, check_vma=False
    )
```

profile of v0, /device:TPU:1, one launch (start us, length us, event | category | flops | bytes accessed | tf_op | source)
XLA Modules:
  0.0 282.5 jit_solution(13694014909298903678)
XLA Ops:
  2.2 1.1 fusion.11
  4.2 25.9 %all_gather.3 = f32[512,64]{1,0:T(8,128)S(1)} all-gather(f32[64,64]{1,0:T(8,128)S(1)} %fusion.9), channel_id=1, replica_groups=mesh['seq'=64,'ch'=8] {'ch'}, dimensions={0}, use_global_device_ids=true | all-gather | bytes 147456 | tf_op jit(solution)/shard_map/all_gather | solution.py:172
  30.8 1.1 fusion.7
  32.6 1.3 reduce
  34.7 16.8 %all-to-all-start.3 = ((f32[64,1,256]{2,1,0:T(1,128)}), f32[64,1,256]{2,1,0:T(1,128)S(1)}, u32[]{:S(2)}, u32[]{:S(2)}) async-start(f32[64,1,256]{2,1,0:T(1,128)} %reshape.995), calls=%async_computation.3 | async-start | bytes 131072 | tf_op jit(solution)/shard_map/all_to_all | solution.py:178
  52.2 4.1 %collective-permute-start = (bf16[32,128]{1,0:T(8,128)(2,1)S(1)}, bf16[32,128]{1,0:T(8,128)(2,1)S(1)}, u32[]{:S(2)}, u32[]{:S(2)}) collective-permute-start(bf16[32,128]{1,0:T(8,128)(2,1)S(1)} %slice.12), channel_id=1, source_target_pairs={{0,8},{8,16},{16,24},{24,32},{32,40},{40,48},{48,56},{56,64},{64,7... | collective-permute-start | bytes 24584 | tf_op jit(solution)/shard_map/ppermute | solution.py:14
  58.5 3.6 %copy.163 = f32[4,8,128,384]{3,1,2,0:T(8,128)S(1)} copy(f32[4,8,128,384]{3,2,1,0:T(8,128)S(1)} %bitcast.127) | data formatting | bytes 12582912
  62.2 3.1 %slice.17 = f32[32,49024]{1,0:T(8,128)} slice(f32[32,49152]{1,0:T(8,128)S(1)} %bitcast.128), slice={[0:32], [0:49024]} | slice | bytes 12550144 | tf_op jit(solution)/shard_map/slice | solution.py:123
  65.3 9.7 %reshape.975 = f32[32,128,383]{2,1,0:T(8,128)} reshape(f32[32,49024]{1,0:T(8,128)} %slice.17) | data formatting | bytes 12550144 | tf_op jit(solution)/shard_map/reshape | solution.py:124
  75.0 4.2 %fusion = f32[32,4,128]{2,1,0:T(4,128)S(1)} fusion(f32[32,128,383]{2,1,0:T(8,128)} %reshape.975, bf16[32,4,128]{2,1,0:T(4,128)(2,1)S(1)} %reshape.974, bf16[32,3,128]{2,1,0:T(4,128)(2,1)S(1)} %bitcast.152, bf16[32,1,128]{2,1,0:T(2,128)(2,1)S(1)} %copy.134), kind=kOutput, calls=%fused_computation | convolution fusion | flops 50528256 | bytes 4325376 | tf_op jit(solution)/shard_map/cij,cbj->cbi/dot_general | solution.py:154
  79.3 1.3 reduce.2
  81.4 9.3 %all-to-all-start = ((f32[64,1,256]{2,1,0:T(1,128)}), f32[64,1,256]{2,1,0:T(1,128)S(1)}, u32[]{:S(2)}, u32[]{:S(2)}) async-start(f32[64,1,256]{2,1,0:T(1,128)} %reshape.989), calls=%async_computation | async-start | bytes 131072 | tf_op jit(solution)/shard_map/all_to_all | solution.py:175
  92.5 7.8 %all-to-all-done = f32[64,1,256]{2,1,0:T(1,128)S(1)} async-done(((f32[64,1,256]{2,1,0:T(1,128)}), f32[64,1,256]{2,1,0:T(1,128)S(1)}, u32[]{:S(2)}, u32[]{:S(2)}) %all-to-all-start) | async-done | bytes 65568 | tf_op jit(solution)/shard_map/all_to_all | solution.py:175
  104.1 4.4 %all-to-all-start.4 = ((f32[64,1,512]{2,1,0:T(1,128)}), f32[64,1,512]{2,1,0:T(1,128)S(1)}, u32[]{:S(2)}, u32[]{:S(2)}) async-start(f32[64,1,512]{2,1,0:T(1,128)} %reshape.999), calls=%async_computation.4 | async-start | bytes 262144 | tf_op jit(solution)/shard_map/all_to_all | solution.py:195
  109.7 9.3 %all-to-all-done.4 = f32[64,1,512]{2,1,0:T(1,128)S(1)} async-done(((f32[64,1,512]{2,1,0:T(1,128)}), f32[64,1,512]{2,1,0:T(1,128)S(1)}, u32[]{:S(2)}, u32[]{:S(2)}) %all-to-all-start.4) | async-done | bytes 131104 | tf_op jit(solution)/shard_map/all_to_all | solution.py:195
  119.0 4.9 %all-to-all-start.5 = ((f32[64,1,512]{2,1,0:T(1,128)}), f32[64,1,512]{2,1,0:T(1,128)S(1)}, u32[]{:S(2)}, u32[]{:S(2)}) async-start(f32[64,1,512]{2,1,0:T(1,128)} %reshape.997), calls=%async_computation.5 | async-start | bytes 262144 | tf_op jit(solution)/shard_map/all_to_all | solution.py:196
  125.1 9.2 %all-to-all-done.5 = f32[64,1,512]{2,1,0:T(1,128)S(1)} async-done(((f32[64,1,512]{2,1,0:T(1,128)}), f32[64,1,512]{2,1,0:T(1,128)S(1)}, u32[]{:S(2)}, u32[]{:S(2)}) %all-to-all-start.5) | async-done | bytes 131104 | tf_op jit(solution)/shard_map/all_to_all | solution.py:196
  134.2 5.2 %all-to-all-start.2 = ((f32[64,1,512]{2,1,0:T(1,128)}), f32[64,1,512]{2,1,0:T(1,128)S(1)}, u32[]{:S(2)}, u32[]{:S(2)}) async-start(f32[64,1,512]{2,1,0:T(1,128)} %reshape.993), calls=%async_computation.2 | async-start | bytes 262144 | tf_op jit(solution)/shard_map/all_to_all | solution.py:194
  141.9 1.7 copy.146
  143.6 1.2 reshape.981
  144.8 1.0 reduce.5
  145.9 1.7 copy.148
  147.7 1.2 reshape.982
  148.9 4.7 %convolution_multiply_fusion = f32[64,512]{1,0:T(8,128)S(1)} fusion(f32[64,512]{1,0:T(8,128)S(1)} %reshape.981), kind=kOutput, calls=%fused_computation.8 | convolution fusion | flops 205029376 | bytes 262144 | tf_op jit(solution)/shard_map/dot_general | solution.py:104
  153.6 10.9 %all-to-all-start.1 = ((f32[64,1,512]{2,1,0:T(1,128)}), f32[64,1,512]{2,1,0:T(1,128)S(1)}, u32[]{:S(2)}, u32[]{:S(2)}) async-start(f32[64,1,512]{2,1,0:T(1,128)} %reshape.991), calls=%async_computation.1 | async-start | bytes 262144 | tf_op jit(solution)/shard_map/all_to_all | solution.py:193
  165.6 1.7 copy.141
  167.4 1.2 reshape.979
  168.6 4.8 %convolution_multiply_fusion.3 = f32[64,512]{1,0:T(8,128)S(1)} fusion(f32[64,512]{1,0:T(8,128)S(1)} %reshape.979), kind=kOutput, calls=%fused_computation.17 | convolution fusion | flops 205029376 | bytes 262144 | tf_op jit(solution)/shard_map/dot_general | solution.py:107
  173.3 5.3 %convolution_multiply_fusion.2 = f32[64,512]{1,0:T(8,128)} fusion(f32[64,512]{1,0:T(8,128)S(1)} %reshape.982), kind=kOutput, calls=%fused_computation.12 | convolution fusion | flops 205029376 | bytes 262144 | tf_op jit(solution)/shard_map/dot_general | solution.py:107
  178.7 4.9 %convolution_add_fusion.1 = f32[64,512]{1,0:T(8,128)S(1)} fusion(f32[64,512]{1,0:T(8,128)S(1)} %convolution_multiply_fusion, f32[64,512]{1,0:T(8,128)S(1)} %reshape.982), kind=kOutput, calls=%fused_computation.9 | convolution fusion | flops 205029376 | bytes 393216 | tf_op jit(solution)/shard_map/dot_general | solution.py:101
  183.6 1.0 reduce.7
  184.7 1.7 copy.139
  186.5 1.2 reshape.978
  187.6 4.7 %convolution_multiply_fusion.1 = f32[64,512]{1,0:T(8,128)S(1)} fusion(f32[64,512]{1,0:T(8,128)S(1)} %reshape.978), kind=kOutput, calls=%fused_computation.10 | convolution fusion | flops 205029376 | bytes 262144 | tf_op jit(solution)/shard_map/dot_general | solution.py:104
  192.4 4.7 %convolution_subtract_fusion.3 = f32[64,512]{1,0:T(8,128)S(1)} fusion(f32[64,512]{1,0:T(8,128)S(1)} %convolution_multiply_fusion.3, f32[64,512]{1,0:T(8,128)S(1)} %reshape.978), kind=kOutput, calls=%fused_computation.18 | convolution fusion | flops 205029376 | bytes 393216 | tf_op jit(solution)/shard_map/dot_general | solution.py:98
  197.1 4.7 %convolution_subtract_fusion.2 = f32[64,512]{1,0:T(8,128)S(1)} fusion(f32[64,512]{1,0:T(8,128)S(1)} %copy-done.4, f32[64,512]{1,0:T(8,128)S(1)} %reshape.981), kind=kOutput, calls=%fused_computation.13 | convolution fusion | flops 205029376 | bytes 393216 | tf_op jit(solution)/shard_map/dot_general | solution.py:98
  201.9 5.0 %multiply_subtract_fusion.1 = (f32[64,512]{1,0:T(8,128)S(1)}, f32[64,512]{1,0:T(8,128)S(1)}) fusion(f32[64,512]{1,0:T(8,128)S(1)} %convolution_add_fusion.1, f32[64,512]{1,0:T(8,128)S(1)} %convolution_subtract_fusion.3, f32[64,512]{1,0:T(8,128)S(1)} %convolution_subtract_fusion.2, f32[64,512]{1,0:T(8,128)S(1)} %convolution_multiply_fusion.1, ...), kind=kOutput, calls=%fused_computation.48 | convolution fusion | flops 205225984 | bytes 917504 | tf_op jit(solution)/shard_map/dot_general | solution.py:101
  206.8 4.7 %fusion.20 = f32[64,512]{1,0:T(8,128)S(1)} fusion(f32[64,512]{1,0:T(8,128)S(1)} %get-tuple-element.6), kind=kOutput, calls=%fused_computation.43 | convolution fusion | flops 204996608 | bytes 262144 | tf_op jit(solution)/shard_map/dot_general | solution.py:101
  211.6 4.7 %fusion.22 = f32[64,512]{1,0:T(8,128)S(1)} fusion(f32[64,512]{1,0:T(8,128)S(1)} %get-tuple-element.5), kind=kOutput, calls=%fused_computation.44 | convolution fusion | flops 204996608 | bytes 262144 | tf_op jit(solution)/shard_map/dot_general | solution.py:98
  216.3 4.8 %convolution_add_fusion = f32[64,512]{1,0:T(8,128)S(1)} fusion(f32[64,512]{1,0:T(8,128)S(1)} %fusion.20, f32[64,512]{1,0:T(8,128)S(1)} %get-tuple-element.5), kind=kOutput, calls=%fused_computation.6 | convolution fusion | flops 205029376 | bytes 393216 | tf_op jit(solution)/shard_map/dot_general | solution.py:104
  221.1 5.0 %convolution_subtract_fusion.1 = f32[64,512]{1,0:T(8,128)S(1)} fusion(f32[64,512]{1,0:T(8,128)S(1)} %fusion.22, f32[64,512]{1,0:T(8,128)S(1)} %get-tuple-element.6), kind=kOutput, calls=%fused_computation.7 | convolution fusion | flops 205029376 | bytes 393216 | tf_op jit(solution)/shard_map/dot_general | solution.py:107
  226.6 1.2 reshape.1001
  227.8 10.3 %all-to-all-start.6 = ((f32[64,1,512]{2,1,0:T(1,128)}), f32[64,1,512]{2,1,0:T(1,128)S(1)}, u32[]{:S(2)}, u32[]{:S(2)}) async-start(f32[64,1,512]{2,1,0:T(1,128)} %reshape.1001), calls=%async_computation.6 | async-start | bytes 262144 | tf_op jit(solution)/shard_map/all_to_all | solution.py:209
  238.3 1.2 reshape.1003
  239.5 8.9 %all-to-all-done.6 = f32[64,1,512]{2,1,0:T(1,128)S(1)} async-done(((f32[64,1,512]{2,1,0:T(1,128)}), f32[64,1,512]{2,1,0:T(1,128)S(1)}, u32[]{:S(2)}, u32[]{:S(2)}) %all-to-all-start.6) | async-done | bytes 131104 | tf_op jit(solution)/shard_map/all_to_all | solution.py:209
  248.4 4.9 %all-to-all-start.7 = ((f32[64,1,512]{2,1,0:T(1,128)}), f32[64,1,512]{2,1,0:T(1,128)S(1)}, u32[]{:S(2)}, u32[]{:S(2)}) async-start(f32[64,1,512]{2,1,0:T(1,128)} %reshape.1003), calls=%async_computation.7 | async-start | bytes 262144 | tf_op jit(solution)/shard_map/all_to_all | solution.py:210
  255.4 8.2 %all-to-all-done.7 = f32[64,1,512]{2,1,0:T(1,128)S(1)} async-done(((f32[64,1,512]{2,1,0:T(1,128)}), f32[64,1,512]{2,1,0:T(1,128)S(1)}, u32[]{:S(2)}, u32[]{:S(2)}) %all-to-all-start.7) | async-done | bytes 131104 | tf_op jit(solution)/shard_map/all_to_all | solution.py:210
  266.1 14.4 %all_to_all.129 = f32[64,1,256]{2,1,0:T(1,128)S(1)} all-to-all(f32[64,1,256]{2,1,0:T(1,128)S(1)} %reshape.1005), channel_id=1, replica_groups=mesh['seq'=64,'ch'=8] {'seq'}, dimensions={0} | all-to-all | bytes 131072 | tf_op jit(solution)/shard_map/all_to_all | solution.py:216
  (102 shorter events, 27.6 us)
Async XLA Ops:
  0.0 3.3 %copy-start = (f32[64,64]{1,0:T(8,128)S(1)}, f32[64,64]{1,0:T(8,128)}, u32[]{:S(2)}) copy-start(f32[64,64]{1,0:T(8,128)} %param.21) | copy-start | bytes 49156
  34.7 46.7 %all-to-all-start.3 = ((f32[64,1,256]{2,1,0:T(1,128)}), f32[64,1,256]{2,1,0:T(1,128)S(1)}, u32[]{:S(2)}, u32[]{:S(2)}) async-start(f32[64,1,256]{2,1,0:T(1,128)} %reshape.995), calls=%async_computation.3 | async-start | bytes 131072 | tf_op jit(solution)/shard_map/all_to_all | solution.py:178
  52.2 22.7 %collective-permute-start = (bf16[32,128]{1,0:T(8,128)(2,1)S(1)}, bf16[32,128]{1,0:T(8,128)(2,1)S(1)}, u32[]{:S(2)}, u32[]{:S(2)}) collective-permute-start(bf16[32,128]{1,0:T(8,128)(2,1)S(1)} %slice.12), channel_id=1, source_target_pairs={{0,8},{8,16},{16,24},{24,32},{32,40},{40,48},{48,56},{56,64},{64,7... | collective-permute-start | bytes 24584 | tf_op jit(solution)/shard_map/ppermute | solution.py:14
  65.3 13.9 %copy-start.1 = (bf16[32,512]{1,0:T(8,128)(2,1)S(1)}, bf16[32,512]{1,0:T(8,128)(2,1)}, u32[]{:S(2)}) copy-start(bf16[32,512]{1,0:T(8,128)(2,1)} %param.13) | copy-start | bytes 98308
  81.4 18.9 %all-to-all-start = ((f32[64,1,256]{2,1,0:T(1,128)}), f32[64,1,256]{2,1,0:T(1,128)S(1)}, u32[]{:S(2)}, u32[]{:S(2)}) async-start(f32[64,1,256]{2,1,0:T(1,128)} %reshape.989), calls=%async_computation | async-start | bytes 131072 | tf_op jit(solution)/shard_map/all_to_all | solution.py:175
  104.1 14.9 %all-to-all-start.4 = ((f32[64,1,512]{2,1,0:T(1,128)}), f32[64,1,512]{2,1,0:T(1,128)S(1)}, u32[]{:S(2)}, u32[]{:S(2)}) async-start(f32[64,1,512]{2,1,0:T(1,128)} %reshape.999), calls=%async_computation.4 | async-start | bytes 262144 | tf_op jit(solution)/shard_map/all_to_all | solution.py:195
  119.0 15.2 %all-to-all-start.5 = ((f32[64,1,512]{2,1,0:T(1,128)}), f32[64,1,512]{2,1,0:T(1,128)S(1)}, u32[]{:S(2)}, u32[]{:S(2)}) async-start(f32[64,1,512]{2,1,0:T(1,128)} %reshape.997), calls=%async_computation.5 | async-start | bytes 262144 | tf_op jit(solution)/shard_map/all_to_all | solution.py:196
  134.2 19.4 %all-to-all-start.2 = ((f32[64,1,512]{2,1,0:T(1,128)}), f32[64,1,512]{2,1,0:T(1,128)S(1)}, u32[]{:S(2)}, u32[]{:S(2)}) async-start(f32[64,1,512]{2,1,0:T(1,128)} %reshape.993), calls=%async_computation.2 | async-start | bytes 262144 | tf_op jit(solution)/shard_map/all_to_all | solution.py:194
  153.6 29.9 %all-to-all-start.1 = ((f32[64,1,512]{2,1,0:T(1,128)}), f32[64,1,512]{2,1,0:T(1,128)S(1)}, u32[]{:S(2)}, u32[]{:S(2)}) async-start(f32[64,1,512]{2,1,0:T(1,128)} %reshape.991), calls=%async_computation.1 | async-start | bytes 262144 | tf_op jit(solution)/shard_map/all_to_all | solution.py:193
  184.7 12.4 %copy-start.4 = (f32[64,512]{1,0:T(8,128)S(1)}, f32[64,512]{1,0:T(8,128)}, u32[]{:S(2)}) copy-start(f32[64,512]{1,0:T(8,128)} %convolution_multiply_fusion.2) | copy-start | bytes 393220
  226.5 55.0 %copy-start.2 = (bf16[32,512]{1,0:T(8,128)(2,1)S(1)}, bf16[32,512]{1,0:T(8,128)(2,1)}, u32[]{:S(2)}) copy-start(bf16[32,512]{1,0:T(8,128)(2,1)} %param.14) | copy-start | bytes 98308
  226.5 55.0 %copy-start.3 = (f32[32]{0:T(128)S(1)}, f32[32]{0:T(128)}, u32[]{:S(2)}) copy-start(f32[32]{0:T(128)} %param.16) | copy-start | bytes 388
  227.8 20.7 %all-to-all-start.6 = ((f32[64,1,512]{2,1,0:T(1,128)}), f32[64,1,512]{2,1,0:T(1,128)S(1)}, u32[]{:S(2)}, u32[]{:S(2)}) async-start(f32[64,1,512]{2,1,0:T(1,128)} %reshape.1001), calls=%async_computation.6 | async-start | bytes 262144 | tf_op jit(solution)/shard_map/all_to_all | solution.py:209
  248.4 15.2 %all-to-all-start.7 = ((f32[64,1,512]{2,1,0:T(1,128)}), f32[64,1,512]{2,1,0:T(1,128)S(1)}, u32[]{:S(2)}, u32[]{:S(2)}) async-start(f32[64,1,512]{2,1,0:T(1,128)} %reshape.1003), calls=%async_computation.7 | async-start | bytes 262144 | tf_op jit(solution)/shard_map/all_to_all | solution.py:210
where the time goes:
time: 287 us; the launch traced here: 283 us
  starting transfers between devices  70.7 us (25%)
  matrix products  67.8 us (24%)
  local copies, waits for them, and re-layouts  44.8 us (16%)
  waiting for transfers between devices  43.4 us (15%)
  blocking collectives  40.4 us (14%)
  other arithmetic  14.5 us (5%)
    all_gather x1, blocking collectives, on_device(): second = lax.all_gather(part_rows, 'ch', axis=0, tiled=True)  25.9 us
    all_to_all x1, starting transfers between devices, on_device(): lax.all_to_all(filter_vals.reshape(channels, 1, local_len), 'seq', split_...  16.8 us
    dot_general x3, matrix products, transform_rows(): jnp.dot(flat_imag, offset_sin, precision=lax.Precision.HIGHEST, preferred...  15.1 us
    dot_general x3, matrix products, transform_rows(): jnp.dot(flat_imag, offset_cos, precision=lax.Precision.HIGHEST, preferred...  14.6 us
    all_to_all x1, blocking collectives, on_device(): lax.all_to_all(result, 'seq', split_axis=1, concat_axis=2, tiled=True)  14.4 us
    unnamed x30, local copies, waits for them, and re-layouts  14.4 us
    dot_general x3, matrix products, transform_rows(): jnp.dot(flat_real, offset_sin, precision=lax.Precision.HIGHEST, preferred...  14.2 us
    dot_general x3, matrix products, transform_rows(): jnp.dot(flat_real, offset_cos, precision=lax.Precision.HIGHEST, preferred...  14.2 us
  transfers between devices with their start and end apart: 9, of which 5 were waited for; matrix products, arithmetic and copies ran while one was open for 24% of the time, Pallas kernels for 0%

commit v1 on v0

v1 whole, which is shorter than its diff:
```python
import functools
import math

import jax
import jax.numpy as jnp
import ml_dtypes
import numpy as np
from jax import lax
from jax.experimental import pallas as pl
from jax.experimental.pallas import tpu as pltpu
from jax.sharding import PartitionSpec as P

MESH = pl.DeviceIdType.MESH
HIGHEST = lax.Precision.HIGHEST
LANES = 128

SINE = (
    25.132741928100586,
    -64.83584594726562,
    67.07760620117188,
    -38.512542724609375,
    14.178224563598633,
    -3.618709087371826,
    0.6094773411750793,
)


def halves(table):
    high = table.astype(ml_dtypes.bfloat16)
    low = (table - high.astype(np.float64)).astype(ml_dtypes.bfloat16)
    return high, low


def tables(full_len):
    rows = full_len // LANES
    rows2 = 2 * rows
    k1 = np.arange(rows)[:, None] + 0.5
    angle = 2.0 * np.pi * k1 * np.arange(rows)[None, :] / rows2
    outer = np.concatenate([np.cos(angle), -np.sin(angle)], axis=0)
    turn = 2.0 * np.pi * k1 * np.arange(LANES)[None, :] / (2 * full_len)
    twiddle = np.stack([np.cos(turn), np.sin(turn)]).astype(np.float32)
    angle = 2.0 * np.pi * (np.outer(np.arange(LANES), np.arange(LANES)) % LANES) / LANES
    inner = np.block([[np.cos(angle), -np.sin(angle)], [np.sin(angle), np.cos(angle)]])
    back = outer.T * (2.0 / (2 * full_len))
    return (
        np.stack(halves(outer)),
        np.stack(halves(inner)),
        np.stack(halves(inner.T)),
        np.stack(halves(back)),
        twiddle,
    )


def sine_of_turns(turns):
    turns = turns - jnp.round(turns)
    square = turns * turns
    total = jnp.full_like(square, SINE[-1])
    for coefficient in SINE[-2::-1]:
        total = total * square + coefficient
    return total * (turns * (0.25 - square))


def split(value):
    high = value.astype(jnp.bfloat16)
    return high, (value - high.astype(jnp.float32)).astype(jnp.bfloat16)


def dot(a, b):
    return jnp.dot(a, b, preferred_element_type=jnp.float32)


def dot3(a, b):
    return dot(a[0], b[0]) + dot(a[0], b[1]) + dot(a[1], b[0])


def dot_first(a, b):
    return lax.dot_general(
        a, b, (((0,), (0,)), ((), ())), precision=HIGHEST, preferred_element_type=jnp.float32
    )


def kernel(
    seq_devs,
    signal,
    in_gate,
    taps,
    skip,
    decay,
    embed_weight,
    embed_bias,
    sine_freq,
    mid_weight,
    mid_bias,
    out_weight,
    outer_hbm,
    inner_hbm,
    inner_back_hbm,
    back_hbm,
    twiddle_hbm,
    result,
    outer,
    inner,
    inner_back,
    back,
    twiddle,
    weight1,
    weight2,
    hidden,
    packed32,
    packed,
    arrived,
    answer,
    answers,
    table_sem,
    send_sem,
    recv_sem,
    back_send_sem,
    back_recv_sem,
):
    channels, local_len = signal.shape
    units = mid_weight.shape[0]
    feats = embed_weight.shape[0]
    per_block = local_len // LANES
    full_len = seq_devs * local_len
    rows = full_len // LANES
    owners = channels
    stride = seq_devs // owners
    me = lax.axis_index("seq")
    mine = me // stride
    owner = me % stride == 0

    barrier = pltpu.get_barrier_semaphore()
    loads = [
        pltpu.make_async_copy(source, target, table_sem.at[index])
        for index, (source, target) in enumerate(
            (
                (outer_hbm, outer),
                (inner_hbm, inner),
                (inner_back_hbm, inner_back),
                (back_hbm, back),
                (twiddle_hbm, twiddle),
            )
        )
    ]

    @pl.when(owner)
    def _():
        def greet(index, carry):
            other = (me + seq_devs - 1 - index) % seq_devs
            pl.semaphore_signal(barrier, inc=1, device_id={"seq": other}, device_id_type=MESH)
            return carry

        lax.fori_loop(0, seq_devs - 1, greet, 0)
        for load in loads:
            load.start()

    row = lax.broadcasted_iota(jnp.int32, weight1.shape[:1] + (local_len,), 0)
    token = me * local_len + lax.broadcasted_iota(jnp.int32, row.shape, 1)
    band = jnp.clip((row - 1) // 2, 0, 15)
    phase = (token << band) & (full_len - 1)
    turns = phase.astype(jnp.float32) * (1.0 / full_len) + jnp.where(row % 2 == 1, 0.25, 0.0)
    place = token.astype(jnp.float32) * (1.0 / full_len)
    features = jnp.where(
        row == 0,
        place,
        jnp.where(row < feats, sine_of_turns(turns), jnp.where(row == feats, 1.0, 0.0)),
    )
    freq = sine_freq[...] * (0.5 / math.pi)
    weight1[...] = jnp.zeros_like(weight1)
    weight1[0:feats, :] = embed_weight[...] * freq
    weight1[feats : feats + 1, :] = embed_bias[...] * freq
    weight2[...] = jnp.zeros_like(weight2)
    weight2[0:units, :] = mid_weight[...] * freq
    weight2[units : units + 1, :] = mid_bias[...] * freq
    hidden[...] = jnp.where(
        lax.broadcasted_iota(jnp.int32, hidden.shape, 0) == units, 1.0, 0.0
    )
    hidden[0:units, :] = sine_of_turns(dot_first(weight1[...], features))
    second = sine_of_turns(dot_first(weight2[...], hidden[...]))
    rate = decay[...]
    raw = dot_first(out_weight[...] * jnp.sqrt(2.0 * rate), second)
    first_row = lax.broadcasted_iota(jnp.int32, (8, local_len), 0) == 0
    times = jnp.where(first_row, token[0:8, :].astype(jnp.float32), 0.0)
    rates = jnp.where(
        lax.broadcasted_iota(jnp.int32, (8, channels), 0) == 0,
        jnp.broadcast_to(rate, (8, channels)),
        0.0,
    )
    filt = raw * jnp.exp(-dot_first(rates, times))
    filt_high = filt.astype(jnp.bfloat16).astype(jnp.float32)

    parts = (
        signal[...].astype(jnp.float32),
        in_gate[...].astype(jnp.float32),
        filt_high,
        filt - filt_high,
    )
    height = len(parts) * per_block
    for kind, part in enumerate(parts):
        for quarter in range(per_block):
            packed32[pl.ds(kind * per_block + quarter, channels, stride=height), :] = part[
                :, quarter * LANES : (quarter + 1) * LANES
            ]
    packed[...] = packed32[...].astype(jnp.bfloat16).reshape(packed.shape)

    @pl.when(owner)
    def _():
        pl.semaphore_wait(barrier, owners - 1)

    @pl.when(jnp.logical_not(owner))
    def _():
        pl.semaphore_wait(barrier, owners)

    def send(index, carry):
        target = (mine + owners // 2 + index) % owners
        device = target * stride

        @pl.when(device == me)
        def _():
            pltpu.make_async_copy(packed.at[target], arrived.at[me], recv_sem).start()

        @pl.when(device != me)
        def _():
            pltpu.make_async_remote_copy(
                src_ref=packed.at[target],
                dst_ref=arrived.at[me],
                send_sem=send_sem,
                recv_sem=recv_sem,
                device_id={"seq": device},
                device_id_type=MESH,
            ).start()

        return carry

    lax.fori_loop(0, owners, send, 0)

    @pl.when(owner)
    def _():
        taps_row = jnp.broadcast_to(taps[pl.ds(mine, 1), :], (LANES, LANES))
        circulant = pltpu.roll(taps_row, 0, 1, stride=1, stride_axis=0)
        source = lax.broadcasted_iota(jnp.int32, (LANES, LANES), 0)
        target = lax.broadcasted_iota(jnp.int32, (LANES, LANES), 1)
        same = target >= source
        toeplitz = jnp.concatenate(
            [jnp.where(same, circulant, 0.0), jnp.where(same, 0.0, circulant)], axis=1
        )
        toeplitz = jnp.concatenate(split(toeplitz), axis=0)
        gain = skip[mine]
        for load in loads:
            load.wait()
        pltpu.make_async_copy(arrived, arrived, recv_sem).wait()

        blocks = arrived[...].astype(jnp.float32).reshape(seq_devs // 2, 2, height, LANES)
        upper = lax.broadcasted_iota(jnp.int32, (seq_devs // 2, 8, LANES), 1) < per_block

        def unpack(pair):
            even = blocks[:, 0, 8 * pair : 8 * pair + 8, :]
            odd = blocks[:, 1, 8 * pair : 8 * pair + 8, :]
            one = jnp.where(upper, even, pltpu.roll(odd, 4, 1))
            two = jnp.where(upper, pltpu.roll(even, 4, 1), odd)
            return one.reshape(rows, LANES), two.reshape(rows, LANES)

        values, gates = unpack(0)
        filter_parts = [part.astype(jnp.bfloat16) for part in unpack(1)]
        values = values.astype(jnp.bfloat16)
        both = dot(jnp.concatenate([values, values], axis=1), toeplitz)
        later = pltpu.roll(both[:, LANES:], 1, 0)
        later = jnp.where(lax.broadcasted_iota(jnp.int32, later.shape, 0) == 0, 0.0, later)
        gated = gates * (both[:, :LANES] + later)

        gated_parts = split(gated)
        columns = [
            jnp.concatenate([g, f], axis=1) for g, f in zip(gated_parts, filter_parts)
        ]
        outer_cols = dot3((outer[0], outer[1]), columns)
        real, imag = outer_cols[:rows, :], outer_cols[rows:, :]
        cosine = jnp.concatenate([twiddle[0], twiddle[0]], axis=1)
        sine = jnp.concatenate([twiddle[1], twiddle[1]], axis=1)
        turned_real = real * cosine + imag * sine
        turned_imag = imag * cosine - real * sine

        def spectrum(lanes):
            joined = jnp.concatenate([turned_real[:, lanes], turned_imag[:, lanes]], axis=1)
            full = dot3(split(joined), (inner[0], inner[1]))
            return full[:, :LANES], full[:, LANES:]

        gated_real, gated_imag = spectrum(slice(0, LANES))
        filt_real, filt_imag = spectrum(slice(LANES, 2 * LANES))
        product = jnp.concatenate(
            [
                gated_real * filt_real - gated_imag * filt_imag,
                gated_real * filt_imag + gated_imag * filt_real,
            ],
            axis=1,
        )
        undone = dot3(split(product), (inner_back[0], inner_back[1]))
        real, imag = undone[:, :LANES], undone[:, LANES:]
        cosine, sine = twiddle[0], twiddle[1]
        stacked = jnp.concatenate(
            [real * cosine - imag * sine, imag * cosine + real * sine], axis=0
        )
        conv = dot3((back[0], back[1]), split(stacked))
        answer[...] = (conv + gain * gated).reshape(answer.shape)

        def reply(index, carry):
            device = (me + seq_devs // 2 + index) % seq_devs

            @pl.when(device == me)
            def _():
                pltpu.make_async_copy(
                    answer.at[device], answers.at[mine], back_recv_sem
                ).start()

            @pl.when(device != me)
            def _():
                pltpu.make_async_remote_copy(
                    src_ref=answer.at[device],
                    dst_ref=answers.at[mine],
                    send_sem=back_send_sem,
                    recv_sem=back_recv_sem,
                    device_id={"seq": device},
                    device_id_type=MESH,
                ).start()

            return carry

        lax.fori_loop(0, seq_devs, reply, 0)

    pltpu.make_async_copy(answers, answers, back_recv_sem).wait()
    for quarter in range(per_block):
        result[:, quarter * LANES : (quarter + 1) * LANES] = answers[:, quarter, :]

    @pl.when(owner)
    def _():
        sent = packed.at[0 : owners - 1]
        pltpu.make_async_copy(sent, sent, send_sem).wait()
        replied = answer.at[0 : seq_devs - 1]
        pltpu.make_async_copy(replied, replied, back_send_sem).wait()

    @pl.when(jnp.logical_not(owner))
    def _():
        pltpu.make_async_copy(packed, packed, send_sem).wait()


def on_device(
    consts,
    signal,
    in_gate,
    out_gate,
    short_taps,
    skip_gain,
    decay_rate,
    embed_weight,
    embed_bias,
    sine_freq,
    mid_weight,
    mid_bias,
    out_weight,
):
    channels, local_len = signal.shape
    seq_devs = lax.axis_size("seq")
    rows = seq_devs * local_len // LANES
    per_block = local_len // LANES
    units = mid_weight.shape[0]
    vmem = pl.BlockSpec(memory_space=pltpu.VMEM)
    smem = pl.BlockSpec(memory_space=pltpu.SMEM)
    hbm = pl.BlockSpec(memory_space=pl.ANY)
    height1 = (embed_weight.shape[0] + 1 + 7) // 8 * 8
    height2 = (units + 1 + 7) // 8 * 8
    result = pl.pallas_call(
        functools.partial(kernel, seq_devs),
        out_shape=jax.ShapeDtypeStruct((channels, local_len), jnp.float32),
        in_specs=[vmem, vmem, vmem, smem] + [vmem] * 7 + [hbm] * 5,
        out_specs=vmem,
        scratch_shapes=[
            *[pltpu.VMEM(const.shape, const.dtype) for const in consts],
            pltpu.VMEM((height1, units), jnp.float32),
            pltpu.VMEM((height2, units), jnp.float32),
            pltpu.VMEM((height2, local_len), jnp.float32),
            pltpu.VMEM((channels * 4 * per_block, LANES), jnp.float32),
            pltpu.VMEM((channels, 4 * per_block, LANES), jnp.bfloat16),
            pltpu.VMEM((seq_devs, 4 * per_block, LANES), jnp.bfloat16),
            pltpu.VMEM((seq_devs, per_block, LANES), jnp.float32),
            pltpu.VMEM((channels, per_block, LANES), jnp.float32),
            pltpu.SemaphoreType.DMA((5,)),
            pltpu.SemaphoreType.DMA,
            pltpu.SemaphoreType.DMA,
            pltpu.SemaphoreType.DMA,
            pltpu.SemaphoreType.DMA,
        ],
        compiler_params=pltpu.CompilerParams(collective_id=0, has_side_effects=True),
    )(
        signal,
        in_gate,
        short_taps,
        skip_gain,
        decay_rate[None, :],
        embed_weight,
        embed_bias[None, :],
        sine_freq[None, :],
        mid_weight,
        mid_bias[None, :],
        out_weight,
        *[jnp.asarray(const) for const in consts],
    )
    return (out_gate.astype(jnp.float32) * result).astype(jnp.bfloat16)


def solution(mesh):
    consts = tables(32768)
    in_specs = (
        P("ch", "seq"),
        P("ch", "seq"),
        P("ch", "seq"),
        P("ch", None),
        P("ch"),
        P("ch"),
        P(),
        P(),
        P(),
        P(),
        P(),
        P(None, "ch"),
    )
    return jax.shard_map(
        functools.partial(on_device, consts),
        mesh=mesh,
        in_specs=in_specs,
        out_specs=P("ch", "seq"),
        check_vma=False,
    )
```

time: 287 us -> 31.6 us (0.11); the launches traced: 283 us -> 31.3 us
  starting transfers between devices: 70.7 us -> 0 us
  matrix products: 67.8 us -> 0 us
  waiting for transfers between devices: 43.4 us -> 0 us
  local copies, waits for them, and re-layouts: 44.8 us -> 1.42 us
  blocking collectives: 40.4 us -> 0 us
  Pallas kernels: 0 us -> 28.4 us
  other arithmetic: 14.5 us -> 1.46 us
    dot_general x22 -> x0, matrix products: 67.8 us -> none  [the longest x3 15.1 us: transform_rows(): jnp.dot(flat_imag, offset_sin, precision=lax.Precision.HIGHEST, preferred...]
    all_to_all x8 -> x0, starting transfers between devices: 66.7 us -> none  [the longest x1 16.8 us: on_device(): lax.all_to_all(filter_vals.reshape(channels, 1, local_len), 'seq', split_...]
    all_to_all x8 -> x0, waiting for transfers between devices: 43.4 us -> none  [the longest x1 9.3 us: on_device(): lax.all_to_all(filt_real, 'seq', split_axis=1, concat_axis=2, tiled=True)]
    pallas_call x0 -> x1, Pallas kernels: none -> 28.4 us  [on_device(): pl.pallas_call(functools.partial(kernel, seq_devs), out_shape=jax.ShapeDt...]
    all_gather x1 -> x0, blocking collectives: 25.9 us -> none  [on_device(): second = lax.all_gather(part_rows, 'ch', axis=0, tiled=True)]
    reshape x12 -> x0, local copies, waits for them, and re-layouts: 15.7 us -> none  [the longest x1 9.68 us: causal_matrix(): return tiled.reshape(channels, tap_count, period - 1)[:, :, :2 * tap_count]]
    all_to_all x1 -> x0, blocking collectives: 14.4 us -> none  [on_device(): lax.all_to_all(result, 'seq', split_axis=1, concat_axis=2, tiled=True)]
    unnamed x30 -> x3, local copies, waits for them, and re-layouts: 14.4 us -> 1.42 us
  transfers between devices with their start and end apart: 9 -> 0, of which waited for: 5 -> 0; matrix products, arithmetic and copies ran while one was open for 24% -> 0% of each run, Pallas kernels for 0% -> 0%
where the time goes in v1:
time: 31.6 us; the launch traced here: 31.3 us
  Pallas kernels  28.4 us (90%)
  other arithmetic  1.46 us (5%)
  local copies, waits for them, and re-layouts  1.42 us (4%)
    pallas_call x1, Pallas kernels, on_device(): pl.pallas_call(functools.partial(kernel, seq_devs), out_shape=jax.ShapeDt...  28.4 us
    convert_element_type x1, other arithmetic, on_device(): return (out_gate.astype(jnp.float32) * result).astype(jnp.bfloat16)  1.46 us
    unnamed x3, local copies, waits for them, and re-layouts  1.42 us

profile of v1, /device:TPU:1, one launch (start us, length us, event | category | flops | bytes accessed | tf_op | source)
XLA Modules:
  0.0 31.3 jit_solution(17621665977802596442)
XLA Ops:
  0.0 1.4 %copy.18.out_weight = f32[64,32]{1,0:T(8,128)} copy(f32[64,32]{0,1:T(8,128)} %param.28) | data formatting | bytes 16384 | tf_op args[11]
  1.4 0.0 copy-start
  1.4 28.4 %shard_map.163 = f32[32,512]{1,0:T(8,128)} custom-call(bf16[32,512]{1,0:T(8,128)(2,1)} %signal.1, bf16[32,512]{1,0:T(8,128)(2,1)} %in_gate.1, f32[32,128]{1,0:T(8,128)} %taps.1, f32[32]{0:T(128)} %skip.1, f32[1,32]{1,0:T(1,128)} %bitcast.4, f32[33,64]{1,0:T(8,128)} %embed_weight.1, f32[1,64]{1,0:T(1,128)} %bitcast.5, f32[1,64]{1,0:T(1,128)} %bitcast.6, ...), custom_call_target="tpu_custom_call" | custom-call | tf_op jit(solution)/shard_map/pallas_call | solution.py:370
  29.8 0.0 copy-done
  29.8 1.5 %multiply_convert_fusion = bf16[32,512]{1,0:T(8,128)(2,1)} fusion(f32[32,512]{1,0:T(8,128)} %shard_map.163, bf16[32,512]{1,0:T(8,128)(2,1)S(1)} %copy-done), kind=kLoop, calls=%fused_computation | loop fusion | flops 49152 | bytes 131072 | tf_op jit(solution)/shard_map/convert_element_type | solution.py:406
Async XLA Ops:
  1.4 28.4 %copy-start = (bf16[32,512]{1,0:T(8,128)(2,1)S(1)}, bf16[32,512]{1,0:T(8,128)(2,1)}, u32[]{:S(2)}) copy-start(bf16[32,512]{1,0:T(8,128)(2,1)} %param.19) | copy-start | bytes 98308

commit v2 on v1

--- a/solution.py
+++ b/solution.py
@@ -73,50 +73,23 @@
     return dot(a[0], b[0]) + dot(a[0], b[1]) + dot(a[1], b[0])
 
 
-def dot_first(a, b):
+def dot_first(a, b, axis=0):
     return lax.dot_general(
-        a, b, (((0,), (0,)), ((), ())), precision=HIGHEST, preferred_element_type=jnp.float32
+        a, b, (((axis,), (0,)), ((), ())), precision=HIGHEST, preferred_element_type=jnp.float32
     )
 
 
 def kernel(
     seq_devs,
-    signal,
-    in_gate,
-    taps,
-    skip,
-    decay,
-    embed_weight,
-    embed_bias,
-    sine_freq,
-    mid_weight,
-    mid_bias,
-    out_weight,
-    outer_hbm,
-    inner_hbm,
-    inner_back_hbm,
-    back_hbm,
-    twiddle_hbm,
-    result,
-    outer,
-    inner,
-    inner_back,
-    back,
-    twiddle,
-    weight1,
-    weight2,
-    hidden,
-    packed32,
-    packed,
-    arrived,
-    answer,
-    answers,
-    table_sem,
-    send_sem,
-    recv_sem,
-    back_send_sem,
-    back_recv_sem,
+    *refs,
 ):
+    sources, refs = refs[:16], refs[16:]
+    result, targets, refs = refs[0], refs[1:17], refs[17:]
+    signal, in_gate, taps, skip, decay = targets[:5]
+    embed_weight, embed_bias, sine_freq, mid_weight, mid_bias, out_weight = targets[5:11]
+    outer, inner, inner_back, back, twiddle = targets[11:]
+    weight1, weight2, hidden, packed32, packed, arrived, answer, answers = refs[:8]
+    load_sem, send_sem, recv_sem, back_send_sem, back_recv_sem = refs[8:]
     channels, local_len = signal.shape
     units = mid_weight.shape[0]
     feats = embed_weight.shape[0]
@@ -131,17 +104,10 @@
 
     barrier = pltpu.get_barrier_semaphore()
     loads = [
-        pltpu.make_async_copy(source, target, table_sem.at[index])
-        for index, (source, target) in enumerate(
-            (
-                (outer_hbm, outer),
-                (inner_hbm, inner),
-                (inner_back_hbm, inner_back),
-                (back_hbm, back),
-                (twiddle_hbm, twiddle),
-            )
-        )
+        pltpu.make_async_copy(source, target, load_sem.at[index])
+        for index, (source, target) in enumerate(zip(sources, targets))
     ]
+    first_loads, weight_loads, owner_loads = loads[:2], loads[4:11], loads[2:4] + loads[11:]
 
     @pl.when(owner)
     def _():
@@ -151,7 +117,13 @@
             return carry
 
         lax.fori_loop(0, seq_devs - 1, greet, 0)
-        for load in loads:
+
+    for load in weight_loads + first_loads:
+        load.start()
+
+    @pl.when(owner)
+    def _():
+        for load in owner_loads:
             load.start()
 
     row = lax.broadcasted_iota(jnp.int32, weight1.shape[:1] + (local_len,), 0)
@@ -165,6 +137,8 @@
         place,
         jnp.where(row < feats, sine_of_turns(turns), jnp.where(row == feats, 1.0, 0.0)),
     )
+    for load in weight_loads:
+        load.wait()
     freq = sine_freq[...] * (0.5 / math.pi)
     weight1[...] = jnp.zeros_like(weight1)
     weight1[0:feats, :] = embed_weight[...] * freq
@@ -178,16 +152,17 @@
     hidden[0:units, :] = sine_of_turns(dot_first(weight1[...], features))
     second = sine_of_turns(dot_first(weight2[...], hidden[...]))
     rate = decay[...]
-    raw = dot_first(out_weight[...] * jnp.sqrt(2.0 * rate), second)
-    first_row = lax.broadcasted_iota(jnp.int32, (8, local_len), 0) == 0
-    times = jnp.where(first_row, token[0:8, :].astype(jnp.float32), 0.0)
-    rates = jnp.where(
-        lax.broadcasted_iota(jnp.int32, (8, channels), 0) == 0,
-        jnp.broadcast_to(rate, (8, channels)),
-        0.0,
-    )
-    filt = raw * jnp.exp(-dot_first(rates, times))
+    raw = dot_first(out_weight[...], second, 1)
+    row = lax.broadcasted_iota(jnp.int32, (8, channels), 0)
+    rates = jnp.broadcast_to(rate, row.shape)
+    rates = jnp.where(row == 0, -rates, jnp.where(row == 1, 0.5 * jnp.log(2.0 * rates), 0.0))
+    row = lax.broadcasted_iota(jnp.int32, (8, local_len), 0)
+    times = jnp.where(row == 0, token[0:8, :].astype(jnp.float32), jnp.where(row == 1, 1.0, 0.0))
+    filt = raw * jnp.exp(dot_first(rates, times))
     filt_high = filt.astype(jnp.bfloat16).astype(jnp.float32)
+
+    for load in first_loads:
+        load.wait()
 
     parts = (
         signal[...].astype(jnp.float32),
@@ -236,6 +211,9 @@
 
     @pl.when(owner)
     def _():
+        for load in owner_loads:
+            load.wait()
+
         taps_row = jnp.broadcast_to(taps[pl.ds(mine, 1), :], (LANES, LANES))
         circulant = pltpu.roll(taps_row, 0, 1, stride=1, stride_axis=0)
         source = lax.broadcasted_iota(jnp.int32, (LANES, LANES), 0)
@@ -245,9 +223,8 @@
             [jnp.where(same, circulant, 0.0), jnp.where(same, 0.0, circulant)], axis=1
         )
         toeplitz = jnp.concatenate(split(toeplitz), axis=0)
-        gain = skip[mine]
-        for load in loads:
-            load.wait()
+        lane = lax.broadcasted_iota(jnp.int32, (1, channels), 1)
+        gain = jnp.sum(jnp.where(lane == mine, skip[...], 0.0), axis=1, keepdims=True)
         pltpu.make_async_copy(arrived, arrived, recv_sem).wait()
 
         blocks = arrived[...].astype(jnp.float32).reshape(seq_devs // 2, 2, height, LANES)
@@ -359,21 +336,32 @@
 ):
     channels, local_len = signal.shape
     seq_devs = lax.axis_size("seq")
-    rows = seq_devs * local_len // LANES
     per_block = local_len // LANES
     units = mid_weight.shape[0]
     vmem = pl.BlockSpec(memory_space=pltpu.VMEM)
-    smem = pl.BlockSpec(memory_space=pltpu.SMEM)
-    hbm = pl.BlockSpec(memory_space=pl.ANY)
+    operands = (
+        signal,
+        in_gate,
+        short_taps,
+        skip_gain[None, :],
+        decay_rate[None, :],
+        embed_weight,
+        embed_bias[None, :],
+        sine_freq[None, :],
+        mid_weight,
+        mid_bias[None, :],
+        out_weight.T,
+        *[jnp.asarray(const) for const in consts],
+    )
     height1 = (embed_weight.shape[0] + 1 + 7) // 8 * 8
     height2 = (units + 1 + 7) // 8 * 8
     result = pl.pallas_call(
         functools.partial(kernel, seq_devs),
-        out_shape=jax.ShapeDtypeStruct((channels, local_len), jnp.float32),
-        in_specs=[vmem, vmem, vmem, smem] + [vmem] * 7 + [hbm] * 5,
+        out_shape=pltpu.VMEM((channels, local_len), jnp.float32),
+        in_specs=[pl.BlockSpec(memory_space=pl.ANY)] * len(operands),
         out_specs=vmem,
         scratch_shapes=[
-            *[pltpu.VMEM(const.shape, const.dtype) for const in consts],
+            *[pltpu.VMEM(operand.shape, operand.dtype) for operand in operands],
             pltpu.VMEM((height1, units), jnp.float32),
             pltpu.VMEM((height2, units), jnp.float32),
             pltpu.VMEM((height2, local_len), jnp.float32),
@@ -382,27 +370,14 @@
             pltpu.VMEM((seq_devs, 4 * per_block, LANES), jnp.bfloat16),
             pltpu.VMEM((seq_devs, per_block, LANES), jnp.float32),
             pltpu.VMEM((channels, per_block, LANES), jnp.float32),
-            pltpu.SemaphoreType.DMA((5,)),
+            pltpu.SemaphoreType.DMA((len(operands),)),
             pltpu.SemaphoreType.DMA,
             pltpu.SemaphoreType.DMA,
             pltpu.SemaphoreType.DMA,
             pltpu.SemaphoreType.DMA,
         ],
         compiler_params=pltpu.CompilerParams(collective_id=0, has_side_effects=True),
-    )(
-        signal,
-        in_gate,
-        short_taps,
-        skip_gain,
-        decay_rate[None, :],
-        embed_weight,
-        embed_bias[None, :],
-        sine_freq[None, :],
-        mid_weight,
-        mid_bias[None, :],
-        out_weight,
-        *[jnp.asarray(const) for const in consts],
-    )
+    )(*operands)
     return (out_gate.astype(jnp.float32) * result).astype(jnp.bfloat16)
 
 

time: 31.6 us -> 28 us (0.89)
  local copies, waits for them, and re-layouts: 1.42 us -> 0.01 us
  Pallas kernels: 28.4 us -> 27.2 us
  other arithmetic: 1.46 us -> 0.62 us
    unnamed x3 -> x2, local copies, waits for them, and re-layouts: 1.42 us -> 0.01 us
    pallas_call x1, Pallas kernels: 28.4 us -> 27.2 us  [on_device(): pl.pallas_call(functools.partial(kernel, seq_devs), out_shape=pltpu.VMEM(...]
    convert_element_type x1, other arithmetic: 1.46 us -> 0.62 us  [on_device(): return (out_gate.astype(jnp.float32) * result).astype(jnp.bfloat16)]
where the time goes in v2:
time: 28 us; the launch traced here: 27.8 us
  Pallas kernels  27.2 us (97%)
  other arithmetic  0.62 us (2%)
    pallas_call x1, Pallas kernels, on_device(): pl.pallas_call(functools.partial(kernel, seq_devs), out_shape=pltpu.VMEM(...  27.2 us
    convert_element_type x1, other arithmetic, on_device(): return (out_gate.astype(jnp.float32) * result).astype(jnp.bfloat16)  0.62 us

profile of v2, /device:TPU:1, one launch (start us, length us, event | category | flops | bytes accessed | tf_op | source)
XLA Modules:
  0.0 27.8 jit_solution(16377125413991900144)
XLA Ops:
  0.0 0.0 copy-start
  0.0 27.2 %shard_map.163 = f32[32,512]{1,0:T(8,128)S(1)} custom-call(bf16[32,512]{1,0:T(8,128)(2,1)} %refs_0_.1, bf16[32,512]{1,0:T(8,128)(2,1)} %refs_1_.1, f32[32,128]{1,0:T(8,128)} %refs_2_.1, f32[1,32]{1,0:T(1,128)} %bitcast.7, f32[1,32]{1,0:T(1,128)} %bitcast.8, f32[33,64]{1,0:T(8,128)} %refs_5_.1, f32[1,64]{1,0:T(1,128)} %bitcast.9, f32[1,64]{1,0:T(1,128)} %bitcast.10, ...), custom_call_target="tpu_custom_call" | custom-call | tf_op jit(solution)/shard_map/pallas_call | solution.py:358
  27.2 0.0 copy-done
  27.2 0.6 %multiply_convert_fusion = bf16[32,512]{1,0:T(8,128)(2,1)} fusion(f32[32,512]{1,0:T(8,128)S(1)} %shard_map.163, bf16[32,512]{1,0:T(8,128)(2,1)S(1)} %copy-done), kind=kLoop, calls=%fused_computation | loop fusion | flops 49152 | bytes 131072 | tf_op jit(solution)/shard_map/convert_element_type | solution.py:381
Async XLA Ops:
  0.0 27.2 %copy-start = (bf16[32,512]{1,0:T(8,128)(2,1)S(1)}, bf16[32,512]{1,0:T(8,128)(2,1)}, u32[]{:S(2)}) copy-start(bf16[32,512]{1,0:T(8,128)(2,1)} %param.19) | copy-start | bytes 98308

commit v3 on v2

--- a/solution.py
+++ b/solution.py
@@ -13,6 +13,8 @@
 MESH = pl.DeviceIdType.MESH
 HIGHEST = lax.Precision.HIGHEST
 LANES = 128
+GRID = (4, 8)
+CORES = 2
 
 SINE = (
     25.132741928100586,
@@ -23,6 +25,14 @@
     -3.618709087371826,
     0.6094773411750793,
 )
+
+
+def far_first():
+    def hops(offset):
+        return sum(min(step, size - step) for step, size in zip(offset, GRID))
+
+    offsets = [(dx, dy) for dx in range(GRID[0]) for dy in range(GRID[1])]
+    return sorted(offsets, key=hops, reverse=True)
 
 
 def halves(table):
@@ -97,10 +107,12 @@
     full_len = seq_devs * local_len
     rows = full_len // LANES
     owners = channels
-    stride = seq_devs // owners
     me = lax.axis_index("seq")
-    mine = me // stride
-    owner = me % stride == 0
+    mine = me // CORES
+    owner = me % CORES == 0
+    by_x = [(mine // GRID[1] + dx) % GRID[0] * GRID[1] for dx in range(GRID[0])]
+    by_y = [(mine % GRID[1] + dy) % GRID[1] for dy in range(GRID[1])]
+    chips = [(by_x[dx] + by_y[dy], dx == dy == 0) for dx, dy in far_first()]
 
     barrier = pltpu.get_barrier_semaphore()
     loads = [
@@ -111,12 +123,14 @@
 
     @pl.when(owner)
     def _():
-        def greet(index, carry):
-            other = (me + seq_devs - 1 - index) % seq_devs
-            pl.semaphore_signal(barrier, inc=1, device_id={"seq": other}, device_id_type=MESH)
-            return carry
-
-        lax.fori_loop(0, seq_devs - 1, greet, 0)
+        for chip, here in chips:
+            for core in range(1 if here else 0, CORES):
+                pl.semaphore_signal(
+                    barrier,
+                    inc=1,
+                    device_id={"seq": chip * CORES + core},
+                    device_id_type=MESH,
+                )
 
     for load in weight_loads + first_loads:
         load.start()
@@ -186,28 +200,27 @@
     def _():
         pl.semaphore_wait(barrier, owners)
 
-    def send(index, carry):
-        target = (mine + owners // 2 + index) % owners
-        device = target * stride
-
-        @pl.when(device == me)
-        def _():
-            pltpu.make_async_copy(packed.at[target], arrived.at[me], recv_sem).start()
-
-        @pl.when(device != me)
-        def _():
-            pltpu.make_async_remote_copy(
-                src_ref=packed.at[target],
-                dst_ref=arrived.at[me],
-                send_sem=send_sem,
-                recv_sem=recv_sem,
-                device_id={"seq": device},
-                device_id_type=MESH,
-            ).start()
-
-        return carry
-
-    lax.fori_loop(0, owners, send, 0)
+    def send(chip):
+        pltpu.make_async_remote_copy(
+            src_ref=packed.at[chip],
+            dst_ref=arrived.at[me],
+            send_sem=send_sem,
+            recv_sem=recv_sem,
+            device_id={"seq": chip * CORES},
+            device_id_type=MESH,
+        ).start()
+
+    for chip, here in chips:
+        if not here:
+            send(chip)
+
+    @pl.when(owner)
+    def _():
+        pltpu.make_async_copy(packed.at[mine], arrived.at[me], recv_sem).start()
+
+    @pl.when(jnp.logical_not(owner))
+    def _():
+        send(mine)
 
     @pl.when(owner)
     def _():
@@ -279,17 +292,9 @@
         conv = dot3((back[0], back[1]), split(stacked))
         answer[...] = (conv + gain * gated).reshape(answer.shape)
 
-        def reply(index, carry):
-            device = (me + seq_devs // 2 + index) % seq_devs
-
-            @pl.when(device == me)
-            def _():
-                pltpu.make_async_copy(
-                    answer.at[device], answers.at[mine], back_recv_sem
-                ).start()
-
-            @pl.when(device != me)
-            def _():
+        for chip, here in chips:
+            for core in range(1 if here else 0, CORES):
+                device = chip * CORES + core
                 pltpu.make_async_remote_copy(
                     src_ref=answer.at[device],
                     dst_ref=answers.at[mine],
@@ -298,10 +303,7 @@
                     device_id={"seq": device},
                     device_id_type=MESH,
                 ).start()
-
-            return carry
-
-        lax.fori_loop(0, seq_devs, reply, 0)
+        pltpu.make_async_copy(answer.at[me], answers.at[mine], back_recv_sem).start()
 
     pltpu.make_async_copy(answers, answers, back_recv_sem).wait()
     for quarter in range(per_block):

time: 28 us -> 25.6 us (0.914)
  Pallas kernels: 27.2 us -> 24.8 us
    pallas_call x1, Pallas kernels: 27.2 us -> 24.8 us  [on_device(): pl.pallas_call(functools.partial(kernel, seq_devs), out_shape=pltpu.VMEM(...]
where the time goes in v3:
time: 25.6 us; the launch traced here: 25.4 us
  Pallas kernels  24.8 us (97%)
  other arithmetic  0.62 us (2%)
    pallas_call x1, Pallas kernels, on_device(): pl.pallas_call(functools.partial(kernel, seq_devs), out_shape=pltpu.VMEM(...  24.8 us
    convert_element_type x1, other arithmetic, on_device(): return (out_gate.astype(jnp.float32) * result).astype(jnp.bfloat16)  0.62 us

profile of v3, /device:TPU:1, one launch (start us, length us, event | category | flops | bytes accessed | tf_op | source)
XLA Modules:
  0.0 25.4 jit_solution(4658744318235156344)
XLA Ops:
  0.0 0.0 copy-start
  0.0 24.8 %shard_map.163 = f32[32,512]{1,0:T(8,128)S(1)} custom-call(bf16[32,512]{1,0:T(8,128)(2,1)} %refs_0_.1, bf16[32,512]{1,0:T(8,128)(2,1)} %refs_1_.1, f32[32,128]{1,0:T(8,128)} %refs_2_.1, f32[1,32]{1,0:T(1,128)} %bitcast.7, f32[1,32]{1,0:T(1,128)} %bitcast.8, f32[33,64]{1,0:T(8,128)} %refs_5_.1, f32[1,64]{1,0:T(1,128)} %bitcast.9, f32[1,64]{1,0:T(1,128)} %bitcast.10, ...), custom_call_target="tpu_custom_call" | custom-call | tf_op jit(solution)/shard_map/pallas_call | solution.py:360
  24.8 0.0 copy-done
  24.8 0.6 %multiply_convert_fusion = bf16[32,512]{1,0:T(8,128)(2,1)} fusion(f32[32,512]{1,0:T(8,128)S(1)} %shard_map.163, bf16[32,512]{1,0:T(8,128)(2,1)S(1)} %copy-done), kind=kLoop, calls=%fused_computation | loop fusion | flops 49152 | bytes 131072 | tf_op jit(solution)/shard_map/convert_element_type | solution.py:383
Async XLA Ops:
  0.0 24.8 %copy-start = (bf16[32,512]{1,0:T(8,128)(2,1)S(1)}, bf16[32,512]{1,0:T(8,128)(2,1)}, u32[]{:S(2)}) copy-start(bf16[32,512]{1,0:T(8,128)(2,1)} %param.19) | copy-start | bytes 98308

commit v4 on v3

--- a/solution.py
+++ b/solution.py
@@ -15,6 +15,8 @@
 LANES = 128
 GRID = (4, 8)
 CORES = 2
+WORK_ROWS = 4
+STAND_IN = GRID[1] * CORES - 1
 
 SINE = (
     25.132741928100586,
@@ -33,6 +35,15 @@
 
     offsets = [(dx, dy) for dx in range(GRID[0]) for dy in range(GRID[1])]
     return sorted(offsets, key=hops, reverse=True)
+
+
+def workers_far_first():
+    def hops(place):
+        dx, near = place
+        return min(dx, GRID[0] - dx) + WORK_ROWS - near
+
+    places = [(dx, near) for dx in range(GRID[0]) for near in range(WORK_ROWS)]
+    return sorted(places, key=hops, reverse=True)
 
 
 def halves(table):
@@ -98,8 +109,10 @@
     signal, in_gate, taps, skip, decay = targets[:5]
     embed_weight, embed_bias, sine_freq, mid_weight, mid_bias, out_weight = targets[5:11]
     outer, inner, inner_back, back, twiddle = targets[11:]
-    weight1, weight2, hidden, packed32, packed, arrived, answer, answers = refs[:8]
-    load_sem, send_sem, recv_sem, back_send_sem, back_recv_sem = refs[8:]
+    weight1, weight2, hidden, packed32, packed_filter32 = refs[:5]
+    packed, packed_filter, arrived, arrived_filter, answer, answers = refs[5:11]
+    load_sem, send_sem, recv_sem, filter_send_sem, filter_recv_sem = refs[11:16]
+    back_send_sem, back_recv_sem = refs[16:]
     channels, local_len = signal.shape
     units = mid_weight.shape[0]
     feats = embed_weight.shape[0]
@@ -107,12 +120,26 @@
     full_len = seq_devs * local_len
     rows = full_len // LANES
     owners = channels
+    share = full_len // owners
     me = lax.axis_index("seq")
-    mine = me // CORES
-    owner = me % CORES == 0
-    by_x = [(mine // GRID[1] + dx) % GRID[0] * GRID[1] for dx in range(GRID[0])]
-    by_y = [(mine % GRID[1] + dy) % GRID[1] for dy in range(GRID[1])]
-    chips = [(by_x[dx] + by_y[dy], dx == dy == 0) for dx, dy in far_first()]
+    chip = me // CORES
+    x, y = chip // GRID[1], chip % GRID[1]
+    by_x = [(x + dx) % GRID[0] for dx in range(GRID[0])]
+    by_y = [(y + dy) % GRID[1] for dy in range(GRID[1])]
+    spare = me == STAND_IN
+    worker = jnp.logical_or(jnp.logical_and(y < WORK_ROWS, me != 0), spare)
+    mine = jnp.where(spare, 0, (x * WORK_ROWS + y) * CORES + me % CORES)
+    others = [
+        (by_x[dx] * GRID[1] + by_y[dy], dx == dy == 0) for dx, dy in far_first()
+    ]
+    upward = (y + 2) // WORK_ROWS % 2
+    workers = []
+    for dx, near in workers_far_first():
+        row = upward * near + (1 - upward) * (WORK_ROWS - 1 - near)
+        for core in range(CORES):
+            device = (by_x[dx] * GRID[1] + row) * CORES + core
+            device = jnp.where(device == 0, STAND_IN, device)
+            workers.append((device, (by_x[dx] * WORK_ROWS + row) * CORES + core))
 
     barrier = pltpu.get_barrier_semaphore()
     loads = [
@@ -121,108 +148,127 @@
     ]
     first_loads, weight_loads, owner_loads = loads[:2], loads[4:11], loads[2:4] + loads[11:]
 
-    @pl.when(owner)
-    def _():
-        for chip, here in chips:
-            for core in range(1 if here else 0, CORES):
-                pl.semaphore_signal(
-                    barrier,
-                    inc=1,
-                    device_id={"seq": chip * CORES + core},
-                    device_id_type=MESH,
-                )
-
-    for load in weight_loads + first_loads:
+    @pl.when(worker)
+    def _():
+        for chip, here in others:
+            for core in range(CORES):
+                device = chip * CORES + core
+
+                def greet(device=device):
+                    pl.semaphore_signal(
+                        barrier, inc=1, device_id={"seq": device}, device_id_type=MESH
+                    )
+
+                if here:
+                    pl.when(device != me)(greet)
+                else:
+                    greet()
+
+    for load in first_loads:
         load.start()
 
-    @pl.when(owner)
-    def _():
-        for load in owner_loads:
+    @pl.when(worker)
+    def _():
+        for load in weight_loads + owner_loads:
             load.start()
-
-    row = lax.broadcasted_iota(jnp.int32, weight1.shape[:1] + (local_len,), 0)
-    token = me * local_len + lax.broadcasted_iota(jnp.int32, row.shape, 1)
-    band = jnp.clip((row - 1) // 2, 0, 15)
-    phase = (token << band) & (full_len - 1)
-    turns = phase.astype(jnp.float32) * (1.0 / full_len) + jnp.where(row % 2 == 1, 0.25, 0.0)
-    place = token.astype(jnp.float32) * (1.0 / full_len)
-    features = jnp.where(
-        row == 0,
-        place,
-        jnp.where(row < feats, sine_of_turns(turns), jnp.where(row == feats, 1.0, 0.0)),
-    )
-    for load in weight_loads:
-        load.wait()
-    freq = sine_freq[...] * (0.5 / math.pi)
-    weight1[...] = jnp.zeros_like(weight1)
-    weight1[0:feats, :] = embed_weight[...] * freq
-    weight1[feats : feats + 1, :] = embed_bias[...] * freq
-    weight2[...] = jnp.zeros_like(weight2)
-    weight2[0:units, :] = mid_weight[...] * freq
-    weight2[units : units + 1, :] = mid_bias[...] * freq
-    hidden[...] = jnp.where(
-        lax.broadcasted_iota(jnp.int32, hidden.shape, 0) == units, 1.0, 0.0
-    )
-    hidden[0:units, :] = sine_of_turns(dot_first(weight1[...], features))
-    second = sine_of_turns(dot_first(weight2[...], hidden[...]))
-    rate = decay[...]
-    raw = dot_first(out_weight[...], second, 1)
-    row = lax.broadcasted_iota(jnp.int32, (8, channels), 0)
-    rates = jnp.broadcast_to(rate, row.shape)
-    rates = jnp.where(row == 0, -rates, jnp.where(row == 1, 0.5 * jnp.log(2.0 * rates), 0.0))
-    row = lax.broadcasted_iota(jnp.int32, (8, local_len), 0)
-    times = jnp.where(row == 0, token[0:8, :].astype(jnp.float32), jnp.where(row == 1, 1.0, 0.0))
-    filt = raw * jnp.exp(dot_first(rates, times))
-    filt_high = filt.astype(jnp.bfloat16).astype(jnp.float32)
 
     for load in first_loads:
         load.wait()
 
-    parts = (
-        signal[...].astype(jnp.float32),
-        in_gate[...].astype(jnp.float32),
-        filt_high,
-        filt - filt_high,
-    )
-    height = len(parts) * per_block
-    for kind, part in enumerate(parts):
-        for quarter in range(per_block):
-            packed32[pl.ds(kind * per_block + quarter, channels, stride=height), :] = part[
-                :, quarter * LANES : (quarter + 1) * LANES
-            ]
+    def spread(target, parts):
+        height = target.shape[0] // channels
+        row = 0
+        for part in parts:
+            for begin in range(0, part.shape[1], LANES):
+                target[pl.ds(row, channels, stride=height), :] = part[:, begin : begin + LANES]
+                row += 1
+
+    spread(packed32, (signal[...].astype(jnp.float32), in_gate[...].astype(jnp.float32)))
     packed[...] = packed32[...].astype(jnp.bfloat16).reshape(packed.shape)
 
-    @pl.when(owner)
-    def _():
+    @pl.when(worker)
+    def _():
+        row = lax.broadcasted_iota(jnp.int32, weight1.shape[:1] + (share,), 0)
+        token = mine * share + lax.broadcasted_iota(jnp.int32, row.shape, 1)
+        band = jnp.clip((row - 1) // 2, 0, 15)
+        phase = (token << band) & (full_len - 1)
+        turns = phase.astype(jnp.float32) * (1.0 / full_len) + jnp.where(row % 2 == 1, 0.25, 0.0)
+        place = token.astype(jnp.float32) * (1.0 / full_len)
+        features = jnp.where(
+            row == 0,
+            place,
+            jnp.where(row < feats, sine_of_turns(turns), jnp.where(row == feats, 1.0, 0.0)),
+        )
+        for load in weight_loads:
+            load.wait()
+        freq = sine_freq[...] * (0.5 / math.pi)
+        weight1[...] = jnp.zeros_like(weight1)
+        weight1[0:feats, :] = embed_weight[...] * freq
+        weight1[feats : feats + 1, :] = embed_bias[...] * freq
+        weight2[...] = jnp.zeros_like(weight2)
+        weight2[0:units, :] = mid_weight[...] * freq
+        weight2[units : units + 1, :] = mid_bias[...] * freq
+        hidden[...] = jnp.where(
+            lax.broadcasted_iota(jnp.int32, hidden.shape, 0) == units, 1.0, 0.0
+        )
+        hidden[0:units, :] = sine_of_turns(dot_first(weight1[...], features))
+        second = sine_of_turns(dot_first(weight2[...], hidden[...]))
+        rate = decay[...]
+        raw = dot_first(out_weight[...], second, 1)
+        row = lax.broadcasted_iota(jnp.int32, (8, channels), 0)
+        rates = jnp.broadcast_to(rate, row.shape)
+        rates = jnp.where(row == 0, -rates, jnp.where(row == 1, 0.5 * jnp.log(2.0 * rates), 0.0))
+        row = lax.broadcasted_iota(jnp.int32, (8, share), 0)
+        times = jnp.where(
+            row == 0, token[0:8, :].astype(jnp.float32), jnp.where(row == 1, 1.0, 0.0)
+        )
+        filt = raw * jnp.exp(dot_first(rates, times))
+        filt_high = filt.astype(jnp.bfloat16).astype(jnp.float32)
+        spread(packed_filter32, (filt_high, filt - filt_high))
+        packed_filter[...] = (
+            packed_filter32[...].astype(jnp.bfloat16).reshape(packed_filter.shape)
+        )
         pl.semaphore_wait(barrier, owners - 1)
 
-    @pl.when(jnp.logical_not(owner))
+    @pl.when(jnp.logical_not(worker))
     def _():
         pl.semaphore_wait(barrier, owners)
 
-    def send(chip):
-        pltpu.make_async_remote_copy(
-            src_ref=packed.at[chip],
-            dst_ref=arrived.at[me],
-            send_sem=send_sem,
-            recv_sem=recv_sem,
-            device_id={"seq": chip * CORES},
-            device_id_type=MESH,
+    for device, index in workers:
+
+        def send(device=device, index=index):
+            pltpu.make_async_remote_copy(
+                src_ref=packed.at[index],
+                dst_ref=arrived.at[me],
+                send_sem=send_sem,
+                recv_sem=recv_sem,
+                device_id={"seq": device},
+                device_id_type=MESH,
+            ).start()
+
+        pl.when(device != me)(send)
+
+    @pl.when(worker)
+    def _():
+        pltpu.make_async_copy(packed.at[mine], arrived.at[me], recv_sem).start()
+        for device, index in workers:
+
+            def send(device=device, index=index):
+                pltpu.make_async_remote_copy(
+                    src_ref=packed_filter.at[index],
+                    dst_ref=arrived_filter.at[mine],
+                    send_sem=filter_send_sem,
+                    recv_sem=filter_recv_sem,
+                    device_id={"seq": device},
+                    device_id_type=MESH,
+                ).start()
+
+            pl.when(device != me)(send)
+        pltpu.make_async_copy(
+            packed_filter.at[mine], arrived_filter.at[mine], filter_recv_sem
         ).start()
 
-    for chip, here in chips:
-        if not here:
-            send(chip)
-
-    @pl.when(owner)
-    def _():
-        pltpu.make_async_copy(packed.at[mine], arrived.at[me], recv_sem).start()
-
-    @pl.when(jnp.logical_not(owner))
-    def _():
-        send(mine)
-
-    @pl.when(owner)
+    @pl.when(worker)
     def _():
         for load in owner_loads:
             load.wait()
@@ -240,18 +286,11 @@
         gain = jnp.sum(jnp.where(lane == mine, skip[...], 0.0), axis=1, keepdims=True)
         pltpu.make_async_copy(arrived, arrived, recv_sem).wait()
 
-        blocks = arrived[...].astype(jnp.float32).reshape(seq_devs // 2, 2, height, LANES)
-        upper = lax.broadcasted_iota(jnp.int32, (seq_devs // 2, 8, LANES), 1) < per_block
-
-        def unpack(pair):
-            even = blocks[:, 0, 8 * pair : 8 * pair + 8, :]
-            odd = blocks[:, 1, 8 * pair : 8 * pair + 8, :]
-            one = jnp.where(upper, even, pltpu.roll(odd, 4, 1))
-            two = jnp.where(upper, pltpu.roll(even, 4, 1), odd)
-            return one.reshape(rows, LANES), two.reshape(rows, LANES)
-
-        values, gates = unpack(0)
-        filter_parts = [part.astype(jnp.bfloat16) for part in unpack(1)]
+        blocks = arrived[...].astype(jnp.float32).reshape(seq_devs // 2, 2, 8, LANES)
+        even, odd = blocks[:, 0], blocks[:, 1]
+        upper = lax.broadcasted_iota(jnp.int32, even.shape, 1) < per_block
+        values = jnp.where(upper, even, pltpu.roll(odd, 4, 1)).reshape(rows, LANES)
+        gates = jnp.where(upper, pltpu.roll(even, 4, 1), odd).reshape(rows, LANES)
         values = values.astype(jnp.bfloat16)
         both = dot(jnp.concatenate([values, values], axis=1), toeplitz)
         later = pltpu.roll(both[:, LANES:], 1, 0)
@@ -259,6 +298,12 @@
         gated = gates * (both[:, :LANES] + later)
 
         gated_parts = split(gated)
+        pltpu.make_async_copy(arrived_filter, arrived_filter, filter_recv_sem).wait()
+        blocks = arrived_filter[...].astype(jnp.float32)
+        filter_parts = [
+            blocks[:, begin : begin + share // LANES].reshape(rows, LANES).astype(jnp.bfloat16)
+            for begin in (0, share // LANES)
+        ]
         columns = [
             jnp.concatenate([g, f], axis=1) for g, f in zip(gated_parts, filter_parts)
         ]
@@ -292,31 +337,40 @@
         conv = dot3((back[0], back[1]), split(stacked))
         answer[...] = (conv + gain * gated).reshape(answer.shape)
 
-        for chip, here in chips:
-            for core in range(1 if here else 0, CORES):
+        for chip, here in others:
+            for core in range(CORES):
                 device = chip * CORES + core
-                pltpu.make_async_remote_copy(
-                    src_ref=answer.at[device],
-                    dst_ref=answers.at[mine],
-                    send_sem=back_send_sem,
-                    recv_sem=back_recv_sem,
-                    device_id={"seq": device},
-                    device_id_type=MESH,
-                ).start()
+
+                def reply(device=device):
+                    pltpu.make_async_remote_copy(
+                        src_ref=answer.at[device],
+                        dst_ref=answers.at[mine],
+                        send_sem=back_send_sem,
+                        recv_sem=back_recv_sem,
+                        device_id={"seq": device},
+                        device_id_type=MESH,
+                    ).start()
+
+                if here:
+                    pl.when(device != me)(reply)
+                else:
+                    reply()
         pltpu.make_async_copy(answer.at[me], answers.at[mine], back_recv_sem).start()
 
     pltpu.make_async_copy(answers, answers, back_recv_sem).wait()
     for quarter in range(per_block):
         result[:, quarter * LANES : (quarter + 1) * LANES] = answers[:, quarter, :]
 
-    @pl.when(owner)
+    @pl.when(worker)
     def _():
         sent = packed.at[0 : owners - 1]
         pltpu.make_async_copy(sent, sent, send_sem).wait()
+        sent = packed_filter.at[0 : owners - 1]
+        pltpu.make_async_copy(sent, sent, filter_send_sem).wait()
         replied = answer.at[0 : seq_devs - 1]
         pltpu.make_async_copy(replied, replied, back_send_sem).wait()
 
-    @pl.when(jnp.logical_not(owner))
+    @pl.when(jnp.logical_not(worker))
     def _():
         pltpu.make_async_copy(packed, packed, send_sem).wait()
 
@@ -339,6 +393,7 @@
     channels, local_len = signal.shape
     seq_devs = lax.axis_size("seq")
     per_block = local_len // LANES
+    share = seq_devs * local_len // channels
     units = mid_weight.shape[0]
     vmem = pl.BlockSpec(memory_space=pltpu.VMEM)
     operands = (
@@ -366,13 +421,18 @@
             *[pltpu.VMEM(operand.shape, operand.dtype) for operand in operands],
             pltpu.VMEM((height1, units), jnp.float32),
             pltpu.VMEM((height2, units), jnp.float32),
-            pltpu.VMEM((height2, local_len), jnp.float32),
-            pltpu.VMEM((channels * 4 * per_block, LANES), jnp.float32),
-            pltpu.VMEM((channels, 4 * per_block, LANES), jnp.bfloat16),
-            pltpu.VMEM((seq_devs, 4 * per_block, LANES), jnp.bfloat16),
+            pltpu.VMEM((height2, share), jnp.float32),
+            pltpu.VMEM((channels * 2 * per_block, LANES), jnp.float32),
+            pltpu.VMEM((channels * 2 * share // LANES, LANES), jnp.float32),
+            pltpu.VMEM((channels, 2 * per_block, LANES), jnp.bfloat16),
+            pltpu.VMEM((channels, 2 * share // LANES, LANES), jnp.bfloat16),
+            pltpu.VMEM((seq_devs, 2 * per_block, LANES), jnp.bfloat16),
+            pltpu.VMEM((channels, 2 * share // LANES, LANES), jnp.bfloat16),
             pltpu.VMEM((seq_devs, per_block, LANES), jnp.float32),
             pltpu.VMEM((channels, per_block, LANES), jnp.float32),
             pltpu.SemaphoreType.DMA((len(operands),)),
+            pltpu.SemaphoreType.DMA,
+            pltpu.SemaphoreType.DMA,
             pltpu.SemaphoreType.DMA,
             pltpu.SemaphoreType.DMA,
             pltpu.SemaphoreType.DMA,

time: 25.6 us -> 24.7 us (0.965)
  Pallas kernels: 24.8 us -> 23.9 us
    pallas_call x1, Pallas kernels: 24.8 us -> 23.9 us  [on_device(): pl.pallas_call(functools.partial(kernel, seq_devs), out_shape=pltpu.VMEM(...]
where the time goes in v4:
time: 24.7 us; the launch traced here: 24.5 us
  Pallas kernels  23.9 us (97%)
  other arithmetic  0.62 us (3%)
    pallas_call x1, Pallas kernels, on_device(): pl.pallas_call(functools.partial(kernel, seq_devs), out_shape=pltpu.VMEM(...  23.9 us
    convert_element_type x1, other arithmetic, on_device(): return (out_gate.astype(jnp.float32) * result).astype(jnp.bfloat16)  0.62 us

profile of v4, /device:TPU:1, one launch (start us, length us, event | category | flops | bytes accessed | tf_op | source)
XLA Modules:
  0.0 24.5 jit_solution(14006050085609590896)
XLA Ops:
  0.0 0.0 copy-start
  0.0 23.9 %shard_map.163 = f32[32,512]{1,0:T(8,128)S(1)} custom-call(bf16[32,512]{1,0:T(8,128)(2,1)} %refs_0_.1, bf16[32,512]{1,0:T(8,128)(2,1)} %refs_1_.1, f32[32,128]{1,0:T(8,128)} %refs_2_.1, f32[1,32]{1,0:T(1,128)} %bitcast.7, f32[1,32]{1,0:T(1,128)} %bitcast.8, f32[33,64]{1,0:T(8,128)} %refs_5_.1, f32[1,64]{1,0:T(1,128)} %bitcast.9, f32[1,64]{1,0:T(1,128)} %bitcast.10, ...), custom_call_target="tpu_custom_call" | custom-call | tf_op jit(solution)/shard_map/pallas_call | solution.py:415
  23.9 0.0 copy-done
  23.9 0.6 %multiply_convert_fusion = bf16[32,512]{1,0:T(8,128)(2,1)} fusion(f32[32,512]{1,0:T(8,128)S(1)} %shard_map.163, bf16[32,512]{1,0:T(8,128)(2,1)S(1)} %copy-done), kind=kLoop, calls=%fused_computation | loop fusion | flops 49152 | bytes 131072 | tf_op jit(solution)/shard_map/convert_element_type | solution.py:443
Async XLA Ops:
  0.0 23.9 %copy-start = (bf16[32,512]{1,0:T(8,128)(2,1)S(1)}, bf16[32,512]{1,0:T(8,128)(2,1)}, u32[]{:S(2)}) copy-start(bf16[32,512]{1,0:T(8,128)(2,1)} %param.19) | copy-start | bytes 98308

commit v5 on v4

--- a/solution.py
+++ b/solution.py
@@ -17,6 +17,8 @@
 CORES = 2
 WORK_ROWS = 4
 STAND_IN = GRID[1] * CORES - 1
+FAR_X = (2, 1, 3, 0)
+REPLY_ROWS = (0, 1, 6, 5, 7, 2, 4, 3)
 
 SINE = (
     25.132741928100586,
@@ -92,6 +94,11 @@
 
 def dot3(a, b):
     return dot(a[0], b[0]) + dot(a[0], b[1]) + dot(a[1], b[0])
+
+
+def dot3_narrow(a, b):
+    both = dot(a[0], jnp.concatenate([b[0], b[1]], axis=1))
+    return both[:, :LANES] + both[:, LANES:] + dot(a[1], b[0])
 
 
 def dot_first(a, b, axis=0):
@@ -284,8 +291,18 @@
         toeplitz = jnp.concatenate(split(toeplitz), axis=0)
         lane = lax.broadcasted_iota(jnp.int32, (1, channels), 1)
         gain = jnp.sum(jnp.where(lane == mine, skip[...], 0.0), axis=1, keepdims=True)
+
+        def spectrum(parts):
+            outer_rows = dot3_narrow((outer[0], outer[1]), parts)
+            real, imag = outer_rows[:rows, :], outer_rows[rows:, :]
+            turned = jnp.concatenate(
+                [real * twiddle[0] + imag * twiddle[1], imag * twiddle[0] - real * twiddle[1]],
+                axis=1,
+            )
+            full = dot3(split(turned), (inner[0], inner[1]))
+            return full[:, :LANES], full[:, LANES:]
+
         pltpu.make_async_copy(arrived, arrived, recv_sem).wait()
-
         blocks = arrived[...].astype(jnp.float32).reshape(seq_devs // 2, 2, 8, LANES)
         even, odd = blocks[:, 0], blocks[:, 1]
         upper = lax.broadcasted_iota(jnp.int32, even.shape, 1) < per_block
@@ -297,30 +314,14 @@
         later = jnp.where(lax.broadcasted_iota(jnp.int32, later.shape, 0) == 0, 0.0, later)
         gated = gates * (both[:, :LANES] + later)
 
-        gated_parts = split(gated)
+        gated_real, gated_imag = spectrum(split(gated))
         pltpu.make_async_copy(arrived_filter, arrived_filter, filter_recv_sem).wait()
         blocks = arrived_filter[...].astype(jnp.float32)
         filter_parts = [
             blocks[:, begin : begin + share // LANES].reshape(rows, LANES).astype(jnp.bfloat16)
             for begin in (0, share // LANES)
         ]
-        columns = [
-            jnp.concatenate([g, f], axis=1) for g, f in zip(gated_parts, filter_parts)
-        ]
-        outer_cols = dot3((outer[0], outer[1]), columns)
-        real, imag = outer_cols[:rows, :], outer_cols[rows:, :]
-        cosine = jnp.concatenate([twiddle[0], twiddle[0]], axis=1)
-        sine = jnp.concatenate([twiddle[1], twiddle[1]], axis=1)
-        turned_real = real * cosine + imag * sine
-        turned_imag = imag * cosine - real * sine
-
-        def spectrum(lanes):
-            joined = jnp.concatenate([turned_real[:, lanes], turned_imag[:, lanes]], axis=1)
-            full = dot3(split(joined), (inner[0], inner[1]))
-            return full[:, :LANES], full[:, LANES:]
-
-        gated_real, gated_imag = spectrum(slice(0, LANES))
-        filt_real, filt_imag = spectrum(slice(LANES, 2 * LANES))
+        filt_real, filt_imag = spectrum(filter_parts)
         product = jnp.concatenate(
             [
                 gated_real * filt_real - gated_imag * filt_imag,
@@ -334,27 +335,28 @@
         stacked = jnp.concatenate(
             [real * cosine - imag * sine, imag * cosine + real * sine], axis=0
         )
-        conv = dot3((back[0], back[1]), split(stacked))
+        conv = dot3_narrow((back[0], back[1]), split(stacked))
         answer[...] = (conv + gain * gated).reshape(answer.shape)
 
-        for chip, here in others:
-            for core in range(CORES):
-                device = chip * CORES + core
-
-                def reply(device=device):
-                    pltpu.make_async_remote_copy(
-                        src_ref=answer.at[device],
-                        dst_ref=answers.at[mine],
-                        send_sem=back_send_sem,
-                        recv_sem=back_recv_sem,
-                        device_id={"seq": device},
-                        device_id_type=MESH,
-                    ).start()
-
-                if here:
-                    pl.when(device != me)(reply)
-                else:
-                    reply()
+        for row in REPLY_ROWS:
+            for dx in FAR_X:
+                for core in range(CORES):
+                    device = (by_x[dx] * GRID[1] + row) * CORES + core
+
+                    def reply(device=device):
+                        pltpu.make_async_remote_copy(
+                            src_ref=answer.at[device],
+                            dst_ref=answers.at[mine],
+                            send_sem=back_send_sem,
+                            recv_sem=back_recv_sem,
+                            device_id={"seq": device},
+                            device_id_type=MESH,
+                        ).start()
+
+                    if dx == 0:
+                        pl.when(device != me)(reply)
+                    else:
+                        reply()
         pltpu.make_async_copy(answer.at[me], answers.at[mine], back_recv_sem).start()
 
     pltpu.make_async_copy(answers, answers, back_recv_sem).wait()

time: 24.7 us -> 23.4 us (0.947)
  Pallas kernels: 23.9 us -> 22.5 us
    pallas_call x1, Pallas kernels: 23.9 us -> 22.5 us  [on_device(): pl.pallas_call(functools.partial(kernel, seq_devs), out_shape=pltpu.VMEM(...]
where the time goes in v5:
time: 23.4 us; the launch traced here: 23.2 us
  Pallas kernels  22.5 us (96%)
  other arithmetic  0.62 us (3%)
    pallas_call x1, Pallas kernels, on_device(): pl.pallas_call(functools.partial(kernel, seq_devs), out_shape=pltpu.VMEM(...  22.5 us
    convert_element_type x1, other arithmetic, on_device(): return (out_gate.astype(jnp.float32) * result).astype(jnp.bfloat16)  0.62 us

profile of v5, /device:TPU:1, one launch (start us, length us, event | category | flops | bytes accessed | tf_op | source)
XLA Modules:
  0.0 23.2 jit_solution(7523054181635861259)
XLA Ops:
  0.0 0.0 copy-start
  0.0 22.5 %shard_map.163 = f32[32,512]{1,0:T(8,128)S(1)} custom-call(bf16[32,512]{1,0:T(8,128)(2,1)} %refs_0_.1, bf16[32,512]{1,0:T(8,128)(2,1)} %refs_1_.1, f32[32,128]{1,0:T(8,128)} %refs_2_.1, f32[1,32]{1,0:T(1,128)} %bitcast.7, f32[1,32]{1,0:T(1,128)} %bitcast.8, f32[33,64]{1,0:T(8,128)} %refs_5_.1, f32[1,64]{1,0:T(1,128)} %bitcast.9, f32[1,64]{1,0:T(1,128)} %bitcast.10, ...), custom_call_target="tpu_custom_call" | custom-call | tf_op jit(solution)/shard_map/pallas_call | solution.py:417
  22.5 0.0 copy-done
  22.5 0.6 %multiply_convert_fusion = bf16[32,512]{1,0:T(8,128)(2,1)} fusion(f32[32,512]{1,0:T(8,128)S(1)} %shard_map.163, bf16[32,512]{1,0:T(8,128)(2,1)S(1)} %copy-done), kind=kLoop, calls=%fused_computation | loop fusion | flops 49152 | bytes 131072 | tf_op jit(solution)/shard_map/convert_element_type | solution.py:445
Async XLA Ops:
  0.0 22.5 %copy-start = (bf16[32,512]{1,0:T(8,128)(2,1)S(1)}, bf16[32,512]{1,0:T(8,128)(2,1)}, u32[]{:S(2)}) copy-start(bf16[32,512]{1,0:T(8,128)(2,1)} %param.19) | copy-start | bytes 98308

commit v6 on v5

--- a/solution.py
+++ b/solution.py
@@ -117,9 +117,9 @@
     embed_weight, embed_bias, sine_freq, mid_weight, mid_bias, out_weight = targets[5:11]
     outer, inner, inner_back, back, twiddle = targets[11:]
     weight1, weight2, hidden, packed32, packed_filter32 = refs[:5]
-    packed, packed_filter, arrived, arrived_filter, answer, answers = refs[5:11]
-    load_sem, send_sem, recv_sem, filter_send_sem, filter_recv_sem = refs[11:16]
-    back_send_sem, back_recv_sem = refs[16:]
+    packed, packed_filter, arrived, arrived_filter, answer = refs[5:10]
+    load_sem, send_sem, recv_sem, filter_send_sem, filter_recv_sem = refs[10:15]
+    back_send_sem, back_recv_sem = refs[15:]
     channels, local_len = signal.shape
     units = mid_weight.shape[0]
     feats = embed_weight.shape[0]
@@ -346,7 +346,7 @@
                     def reply(device=device):
                         pltpu.make_async_remote_copy(
                             src_ref=answer.at[device],
-                            dst_ref=answers.at[mine],
+                            dst_ref=result.at[mine],
                             send_sem=back_send_sem,
                             recv_sem=back_recv_sem,
                             device_id={"seq": device},
@@ -357,11 +357,9 @@
                         pl.when(device != me)(reply)
                     else:
                         reply()
-        pltpu.make_async_copy(answer.at[me], answers.at[mine], back_recv_sem).start()
-
-    pltpu.make_async_copy(answers, answers, back_recv_sem).wait()
-    for quarter in range(per_block):
-        result[:, quarter * LANES : (quarter + 1) * LANES] = answers[:, quarter, :]
+        pltpu.make_async_copy(answer.at[me], result.at[mine], back_recv_sem).start()
+
+    pltpu.make_async_copy(result, result, back_recv_sem).wait()
 
     @pl.when(worker)
     def _():
@@ -416,7 +414,7 @@
     height2 = (units + 1 + 7) // 8 * 8
     result = pl.pallas_call(
         functools.partial(kernel, seq_devs),
-        out_shape=pltpu.VMEM((channels, local_len), jnp.float32),
+        out_shape=pltpu.VMEM((channels, per_block, LANES), jnp.float32),
         in_specs=[pl.BlockSpec(memory_space=pl.ANY)] * len(operands),
         out_specs=vmem,
         scratch_shapes=[
@@ -431,7 +429,6 @@
             pltpu.VMEM((seq_devs, 2 * per_block, LANES), jnp.bfloat16),
             pltpu.VMEM((channels, 2 * share // LANES, LANES), jnp.bfloat16),
             pltpu.VMEM((seq_devs, per_block, LANES), jnp.float32),
-            pltpu.VMEM((channels, per_block, LANES), jnp.float32),
             pltpu.SemaphoreType.DMA((len(operands),)),
             pltpu.SemaphoreType.DMA,
             pltpu.SemaphoreType.DMA,
@@ -442,6 +439,7 @@
         ],
         compiler_params=pltpu.CompilerParams(collective_id=0, has_side_effects=True),
     )(*operands)
+    result = result.reshape(channels, local_len)
     return (out_gate.astype(jnp.float32) * result).astype(jnp.bfloat16)
 
 

time: 23.4 us -> 23.3 us (level)
  no operation moved by 1% of the time
where the time goes in v6:
time: 23.3 us; the launch traced here: 23.1 us
  Pallas kernels  22.5 us (97%)
  other arithmetic  0.62 us (3%)
    pallas_call x1, Pallas kernels, on_device(): pl.pallas_call(functools.partial(kernel, seq_devs), out_shape=pltpu.VMEM(...  22.5 us
    convert_element_type x1, other arithmetic, on_device(): return (out_gate.astype(jnp.float32) * result).astype(jnp.bfloat16)  0.62 us

profile of v6, /device:TPU:1, one launch (start us, length us, event | category | flops | bytes accessed | tf_op | source)
XLA Modules:
  0.0 23.1 jit_solution(11171716804205286888)
XLA Ops:
  0.0 0.0 copy-start
  0.0 22.5 %shard_map.163 = f32[32,4,128]{2,1,0:T(4,128)S(1)} custom-call(bf16[32,512]{1,0:T(8,128)(2,1)} %refs_0_.1, bf16[32,512]{1,0:T(8,128)(2,1)} %refs_1_.1, f32[32,128]{1,0:T(8,128)} %refs_2_.1, f32[1,32]{1,0:T(1,128)} %bitcast.13, f32[1,32]{1,0:T(1,128)} %bitcast.14, f32[33,64]{1,0:T(8,128)} %refs_5_.1, f32[1,64]{1,0:T(1,128)} %bitcast.15, f32[1,64]{1,0:T(1,128)} %bitcast.16, ...), custom_call_target="tpu_custom_call" | custom-call | tf_op jit(solution)/shard_map/pallas_call | solution.py:415
  22.5 0.0 copy-done
  22.5 0.6 %fusion = bf16[32,512]{1,0:T(8,128)(2,1)} fusion(f32[4,8,4,128]{3,2,1,0:T(4,128)S(1)} %bitcast.11, bf16[32,512]{1,0:T(8,128)(2,1)S(1)} %copy-done), kind=kLoop, calls=%fused_computation.1 | loop fusion | flops 49152 | bytes 131072 | tf_op jit(solution)/shard_map/convert_element_type | solution.py:443
Async XLA Ops:
  0.0 22.5 %copy-start = (bf16[32,512]{1,0:T(8,128)(2,1)S(1)}, bf16[32,512]{1,0:T(8,128)(2,1)}, u32[]{:S(2)}) copy-start(bf16[32,512]{1,0:T(8,128)(2,1)} %param.19) | copy-start | bytes 98308

commit v7 on v6

--- a/solution.py
+++ b/solution.py
@@ -18,6 +18,7 @@
 WORK_ROWS = 4
 STAND_IN = GRID[1] * CORES - 1
 FAR_X = (2, 1, 3, 0)
+GREET_FIRST = 10
 REPLY_ROWS = (0, 1, 6, 5, 7, 2, 4, 3)
 
 SINE = (
@@ -146,7 +147,7 @@
         for core in range(CORES):
             device = (by_x[dx] * GRID[1] + row) * CORES + core
             device = jnp.where(device == 0, STAND_IN, device)
-            workers.append((device, (by_x[dx] * WORK_ROWS + row) * CORES + core))
+            workers.append((device, (by_x[dx] * WORK_ROWS + row) * CORES + core, dx == 0))
 
     barrier = pltpu.get_barrier_semaphore()
     loads = [
@@ -155,28 +156,29 @@
     ]
     first_loads, weight_loads, owner_loads = loads[:2], loads[4:11], loads[2:4] + loads[11:]
 
+    def greet(device):
+        pl.semaphore_signal(barrier, inc=1, device_id={"seq": device}, device_id_type=MESH)
+
     @pl.when(worker)
     def _():
-        for chip, here in others:
+        for chip, here in others[:GREET_FIRST]:
+            for core in range(CORES):
+                greet(chip * CORES + core)
+        for load in weight_loads + first_loads:
+            load.start()
+        for chip, here in others[GREET_FIRST:]:
             for core in range(CORES):
                 device = chip * CORES + core
-
-                def greet(device=device):
-                    pl.semaphore_signal(
-                        barrier, inc=1, device_id={"seq": device}, device_id_type=MESH
-                    )
-
                 if here:
-                    pl.when(device != me)(greet)
+                    pl.when(device != me)(functools.partial(greet, device))
                 else:
-                    greet()
-
-    for load in first_loads:
-        load.start()
-
-    @pl.when(worker)
-    def _():
-        for load in weight_loads + owner_loads:
+                    greet(device)
+        for load in owner_loads:
+            load.start()
+
+    @pl.when(jnp.logical_not(worker))
+    def _():
+        for load in first_loads:
             load.start()
 
     for load in first_loads:
@@ -241,7 +243,7 @@
     def _():
         pl.semaphore_wait(barrier, owners)
 
-    for device, index in workers:
+    for device, index, near in workers:
 
         def send(device=device, index=index):
             pltpu.make_async_remote_copy(
@@ -253,12 +255,12 @@
                 device_id_type=MESH,
             ).start()
 
-        pl.when(device != me)(send)
+        pl.when(device != me)(send) if near else send()
 
     @pl.when(worker)
     def _():
         pltpu.make_async_copy(packed.at[mine], arrived.at[me], recv_sem).start()
-        for device, index in workers:
+        for device, index, near in workers:
 
             def send(device=device, index=index):
                 pltpu.make_async_remote_copy(
@@ -270,7 +272,7 @@
                     device_id_type=MESH,
                 ).start()
 
-            pl.when(device != me)(send)
+            pl.when(device != me)(send) if near else send()
         pltpu.make_async_copy(
             packed_filter.at[mine], arrived_filter.at[mine], filter_recv_sem
         ).start()

time: 23.3 us -> 23.3 us (level)
  no operation moved by 1% of the time
where the time goes in v7:
time: 23.3 us; the launch traced here: 23.1 us
  Pallas kernels  22.5 us (97%)
  other arithmetic  0.62 us (3%)
    pallas_call x1, Pallas kernels, on_device(): pl.pallas_call(functools.partial(kernel, seq_devs), out_shape=pltpu.VMEM(...  22.5 us
    convert_element_type x1, other arithmetic, on_device(): return (out_gate.astype(jnp.float32) * result).astype(jnp.bfloat16)  0.62 us

profile of v7, /device:TPU:1, one launch (start us, length us, event | category | flops | bytes accessed | tf_op | source)
XLA Modules:
  0.0 23.1 jit_solution(10987866571561619840)
XLA Ops:
  0.0 0.0 copy-start
  0.0 22.5 %shard_map.163 = f32[32,4,128]{2,1,0:T(4,128)S(1)} custom-call(bf16[32,512]{1,0:T(8,128)(2,1)} %refs_0_.1, bf16[32,512]{1,0:T(8,128)(2,1)} %refs_1_.1, f32[32,128]{1,0:T(8,128)} %refs_2_.1, f32[1,32]{1,0:T(1,128)} %bitcast.13, f32[1,32]{1,0:T(1,128)} %bitcast.14, f32[33,64]{1,0:T(8,128)} %refs_5_.1, f32[1,64]{1,0:T(1,128)} %bitcast.15, f32[1,64]{1,0:T(1,128)} %bitcast.16, ...), custom_call_target="tpu_custom_call" | custom-call | tf_op jit(solution)/shard_map/pallas_call | solution.py:417
  22.5 0.0 copy-done
  22.5 0.6 %fusion = bf16[32,512]{1,0:T(8,128)(2,1)} fusion(f32[4,8,4,128]{3,2,1,0:T(4,128)S(1)} %bitcast.11, bf16[32,512]{1,0:T(8,128)(2,1)S(1)} %copy-done), kind=kLoop, calls=%fused_computation.1 | loop fusion | flops 49152 | bytes 131072 | tf_op jit(solution)/shard_map/convert_element_type | solution.py:445
Async XLA Ops:
  0.0 22.5 %copy-start = (bf16[32,512]{1,0:T(8,128)(2,1)S(1)}, bf16[32,512]{1,0:T(8,128)(2,1)}, u32[]{:S(2)}) copy-start(bf16[32,512]{1,0:T(8,128)(2,1)} %param.19) | copy-start | bytes 98308
